TPU v7x, 256 devices: a whole 4x4x8 slice. The times are simulated.
256 devices in a mesh: dp: 8 (over x, z_hi), expert: 32 (over z_lo, y, core).
Axes of the slice: x: 4, y: 4, z: 8 (z_hi: 2, z_lo: 4; z = z_hi * 4 + z_lo), core: 2. Of those that a mesh axis runs over, the one named last changes fastest.
Arguments:
- tokens: bfloat16 [32768, 5120], P(('dp', 'expert')), may hold values from -6 to 6
- cotangent: bfloat16 [32768, 5120], P(('dp', 'expert')), may hold values from -2 to 2
- picks: int32 [256, 32, 4], P(('dp', 'expert')), may hold values from 0 to 127, as said below
- gates: float32 [256, 32, 4], P(('dp', 'expert')), may hold values from 0.05 to 1
- w_gate: bfloat16 [32, 5120, 768], P('expert', 'dp'), may hold values from -0.078125 to 0.078125
- w_up: bfloat16 [32, 5120, 768], P('expert', 'dp'), may hold values from -0.078125 to 0.078125
- w_down: bfloat16 [32, 768, 5120], P('expert', None, 'dp'), may hold values from -0.21875 to 0.21875
Outputs:
- mixed: bfloat16 [32768, 5120], P(('dp', 'expert'))
- token_grad: bfloat16 [32768, 5120], P(('dp', 'expert'))
- gate_grad: float32 [256, 32, 4], P(('dp', 'expert'))
- grad_w_gate: bfloat16 [32, 5120, 768], P('expert', 'dp')
- grad_w_up: bfloat16 [32, 5120, 768], P('expert', 'dp')
- grad_w_down: bfloat16 [32, 768, 5120], P('expert', None, 'dp')
Inputs may be any that keep to these rules, and one draw needn't show every extreme that they name: picks[d, e] holds 4 distinct token indices of device d; every expert takes exactly 4 tokens from every device.
All inputs are finite; a program needn't handle non-finite values.
Results may differ from a plain program's by a relative error of at most 0.02.
Values may be sent and summed in bfloat16 or wider, within the bound.
A program may use at most 64 MiB of HBM per device.

v0:
```python
import jax
import jax.numpy as jnp
from jax import lax
from jax.sharding import PartitionSpec as P


def contract_rows(left, right):
    return lax.dot_general(
        left, right, (((0,), (0,)), ((), ())), preferred_element_type=jnp.float32
    )


def contract_cols(left, right):
    return lax.dot_general(
        left, right, (((1,), (1,)), ((), ())), preferred_element_type=jnp.float32
    )


def rounded(values):
    return lax.optimization_barrier(values.astype(jnp.bfloat16)).astype(jnp.float32)


def swiglu_grads(column_sums, hidden_units):
    gate_sum = column_sums[:, :hidden_units]
    up_sum = column_sums[:, hidden_units : 2 * hidden_units]
    back_sum = column_sums[:, 2 * hidden_units :]
    sigmoid_gate = jax.nn.sigmoid(gate_sum)
    silu_gate = gate_sum * sigmoid_gate
    hidden = (silu_gate * up_sum).astype(jnp.bfloat16)
    grad_up = (back_sum * silu_gate).astype(jnp.bfloat16)
    grad_gate = (back_sum * up_sum * sigmoid_gate * (1.0 + gate_sum * (1.0 - sigmoid_gate))).astype(
        jnp.bfloat16
    )
    return (hidden, grad_gate, grad_up)


def body(tokens, cotangent, picks, gates, w_gate, w_up, w_down):
    expert_count = picks.shape[1]
    slot_count = picks.shape[2]
    model_width = tokens.shape[1]
    chosen = picks[0].reshape(-1)
    scales = gates[0].reshape(-1)
    token_rows = jnp.take(tokens, chosen, axis=0)
    grad_rows = jnp.take(cotangent, chosen, axis=0)
    scaled_grad = (scales[:, None] * grad_rows.astype(jnp.float32)).astype(jnp.bfloat16)
    outgoing = (
        token_rows.reshape(expert_count, slot_count, model_width),
        scaled_grad.reshape(expert_count, slot_count, model_width),
    )
    arrived_in, arrived_up = (
        lax.all_to_all(
            lax.all_to_all(outgoing[0], "dp", split_axis=2, concat_axis=1, tiled=True),
            "expert",
            split_axis=0,
            concat_axis=0,
            tiled=True,
        ),
        lax.all_to_all(
            lax.all_to_all(outgoing[1], "dp", split_axis=2, concat_axis=1, tiled=True),
            "expert",
            split_axis=0,
            concat_axis=0,
            tiled=True,
        ),
    )
    arrived_shape = arrived_in.shape
    row_count = arrived_shape[0] * arrived_shape[1]
    slice_width = arrived_shape[2]
    inputs = arrived_in.reshape(row_count, slice_width)
    upstream = arrived_up.reshape(row_count, slice_width)
    gate_mat = w_gate[0]
    up_mat = w_up[0]
    down_mat = w_down[0]
    hidden_units = gate_mat.shape[1]
    terms = jnp.concatenate(
        [
            rounded(jnp.dot(inputs, gate_mat, preferred_element_type=jnp.float32)),
            rounded(jnp.dot(inputs, up_mat, preferred_element_type=jnp.float32)),
            rounded(contract_cols(upstream, down_mat)),
        ],
        axis=1,
    )
    shares = lax.psum_scatter(
        terms.astype(jnp.bfloat16), "dp", scatter_dimension=0, tiled=True
    ).astype(jnp.float32)
    own_hidden, own_grad_gate, own_grad_up = swiglu_grads(shares, hidden_units)
    hidden, grad_gate, grad_up = (
        lax.all_gather(own_hidden, "dp", axis=0, tiled=True),
        lax.all_gather(own_grad_gate, "dp", axis=0, tiled=True),
        lax.all_gather(own_grad_up, "dp", axis=0, tiled=True),
    )
    expert_out = jnp.dot(hidden, down_mat, preferred_element_type=jnp.float32).astype(jnp.bfloat16)
    input_grad = (contract_cols(grad_gate, gate_mat) + contract_cols(grad_up, up_mat)).astype(
        jnp.bfloat16
    )
    grad_down = contract_rows(hidden, upstream).astype(jnp.bfloat16)[None]
    grad_gate_w = contract_rows(inputs, grad_gate).astype(jnp.bfloat16)[None]
    grad_up_w = contract_rows(inputs, grad_up).astype(jnp.bfloat16)[None]
    back_out, back_grad = (
        lax.all_to_all(
            lax.all_to_all(
                expert_out.reshape(arrived_shape), "dp", split_axis=1, concat_axis=2, tiled=True
            ),
            "expert",
            split_axis=0,
            concat_axis=0,
            tiled=True,
        ),
        lax.all_to_all(
            lax.all_to_all(
                input_grad.reshape(arrived_shape), "dp", split_axis=1, concat_axis=2, tiled=True
            ),
            "expert",
            split_axis=0,
            concat_axis=0,
            tiled=True,
        ),
    )
    back_out = back_out.reshape(expert_count * slot_count, model_width)
    back_grad = back_grad.reshape(expert_count * slot_count, model_width)
    positions = jnp.arange(tokens.shape[0], dtype=jnp.int32)
    select = chosen[:, None] == positions[None, :]
    weighted = jnp.where(select, scales[:, None], jnp.float32(0.0))
    out_float = back_out.astype(jnp.float32)
    mixed = lax.dot_general(
        weighted,
        out_float,
        (((0,), (0,)), ((), ())),
        precision=lax.Precision.HIGHEST,
        preferred_element_type=jnp.float32,
    ).astype(jnp.bfloat16)
    token_grad = contract_rows(select.astype(jnp.bfloat16), back_grad).astype(jnp.bfloat16)
    gate_grad = jnp.sum(grad_rows.astype(jnp.float32) * out_float, axis=1).reshape(
        1, expert_count, slot_count
    )
    return (mixed, token_grad, gate_grad, grad_gate_w, grad_up_w, grad_down)


def solution(mesh):
    return jax.shard_map(
        body,
        mesh=mesh,
        in_specs=(
            P(("dp", "expert"), None),
            P(("dp", "expert"), None),
            P(("dp", "expert"), None, None),
            P(("dp", "expert"), None, None),
            P("expert", "dp", None),
            P("expert", "dp", None),
            P("expert", None, "dp"),
        ),
        out_specs=(
            P(("dp", "expert"), None),
            P(("dp", "expert"), None),
            P(("dp", "expert"), None, None),
            P("expert", "dp", None),
            P("expert", "dp", None),
            P("expert", None, "dp"),
        ),
        check_vma=False,
    )
```

profile of v0, /device:TPU:1, one launch (start us, length us, event | category | flops | bytes accessed | tf_op | source)
XLA Modules:
  0.0 669.7 jit_solution(6501620156101534513)
XLA Ops:
  12.1 8.8 %copy.79 = bf16[32,4,5120]{0,1,2:T(4,128)(2,1)} copy(bf16[32,4,5120]{2,1,0:T(4,128)(2,1)} %reshape.48) | data formatting | bytes 2621440 | tf_op jit(solution)/shard_map/reshape | solution.py:48
  20.9 8.6 %reshape.77 = bf16[8,2,40960]{2,1,0:T(2,128)(2,1)} reshape(bf16[5120,4,32]{2,1,0:T(4,128)(2,1)} %bitcast.66) | data formatting | bytes 2621440
  29.5 11.6 %all-to-all-start.2 = ((bf16[8,2,40960]{2,1,0:T(2,128)(2,1)}), bf16[8,2,40960]{2,1,0:T(2,128)(2,1)}, u32[]{:S(2)}, u32[]{:S(2)}) async-start(bf16[8,2,40960]{2,1,0:T(2,128)(2,1)} %reshape.77), calls=%async_computation.2 | async-start | bytes 2621440 | tf_op jit(solution)/shard_map/all_to_all | solution.py:59
  41.1 2.4 gather_fusion
  43.5 1.5 broadcast_select_fusion.1
  46.3 8.8 %copy.75 = bf16[32,4,5120]{0,1,2:T(4,128)(2,1)} copy(bf16[32,4,5120]{2,1,0:T(4,128)(2,1)} %reshape.46) | data formatting | bytes 2621440 | tf_op jit(solution)/shard_map/reshape | solution.py:47
  55.1 8.7 %reshape.79 = bf16[8,2,40960]{2,1,0:T(2,128)(2,1)} reshape(bf16[5120,4,32]{2,1,0:T(4,128)(2,1)} %bitcast.67) | data formatting | bytes 2621440
  63.7 2.6 all-to-all-done.2
  66.3 6.5 all-to-all-start
  72.8 7.5 %reshape.78 = bf16[5120,4,32]{2,1,0:T(4,128)(2,1)} reshape(bf16[8,2,40960]{2,1,0:T(2,128)(2,1)} %all-to-all-done.2) | data formatting | bytes 2621440
  80.3 7.1 %copy.92 = bf16[32,4,8,640]{3,0,1,2:T(8,128)(2,1)} copy(bf16[32,4,8,640]{0,1,3,2:T(4,128)(2,1)} %bitcast.68) | data formatting | bytes 2621440 | tf_op jit(solution)/shard_map/all_to_all | solution.py:59
  87.4 2.8 copy.82
  90.2 3.4 all-to-all-done
  93.6 23.1 %all-to-all-start.3 = ((bf16[32,32,640]{2,1,0:T(8,128)(2,1)}), bf16[32,32,640]{2,1,0:T(8,128)(2,1)}, u32[]{:S(2)}, u32[]{:S(2)}) async-start(bf16[32,32,640]{2,1,0:T(8,128)(2,1)} %copy.82), calls=%async_computation.3 | async-start | bytes 2621440 | tf_op jit(solution)/shard_map/all_to_all | solution.py:58
  116.7 5.0 reshape.80
  121.7 6.0 copy.90
  129.2 19.3 %all-to-all-done.3 = bf16[32,32,640]{2,1,0:T(8,128)(2,1)} async-done(((bf16[32,32,640]{2,1,0:T(8,128)(2,1)}), bf16[32,32,640]{2,1,0:T(8,128)(2,1)}, u32[]{:S(2)}, u32[]{:S(2)}) %all-to-all-start.3) | async-done | bytes 1310752 | tf_op jit(solution)/shard_map/all_to_all | solution.py:58
  148.5 5.6 all-to-all-start.1
  154.2 4.2 convolution_convert_fusion.2
  158.4 27.5 %all-to-all-done.1 = bf16[32,32,640]{2,1,0:T(8,128)(2,1)S(1)} async-done(((bf16[32,32,640]{2,1,0:T(8,128)(2,1)}), bf16[32,32,640]{2,1,0:T(8,128)(2,1)S(1)}, u32[]{:S(2)}, u32[]{:S(2)}) %all-to-all-start.1) | async-done | bytes 1310752 | tf_op jit(solution)/shard_map/all_to_all | solution.py:51
  185.9 3.1 convolution_convert_fusion.3
  190.4 2.3 pad_maximum_fusion
  192.8 125.2 %reduce-scatter.2.cloned.1.call-done = bf16[128,2304]{1,0:T(8,128)(2,1)} async-done(((bf16[1024,2304]{1,0:T(8,128)(2,1)}), bf16[128,2304]{1,0:T(8,128)(2,1)}) %reduce-scatter.2.cloned.1.call-update) | async-done | bytes 589840 | tf_op jit(solution)/shard_map/reduce_scatter | solution.py:83
  321.5 62.8 %all-gather.4.cloned.1.call-done = bf16[1024,768]{1,0:T(8,128)(2,1)} async-done(((bf16[128,768]{1,0:T(8,128)(2,1)}), bf16[1024,768]{1,0:T(8,128)(2,1)}) %all-gather.4.cloned.1.call-update) | async-done | bytes 1572880 | tf_op jit(solution)/shard_map/all_gather | solution.py:88
  384.3 3.1 convolution_convert_fusion.5
  388.8 3.7 all-to-all-start.4
  392.5 74.9 %all-gather.6.cloned.1.call-done = bf16[1024,768]{1,0:T(8,128)(2,1)} async-done(((bf16[128,768]{1,0:T(8,128)(2,1)}), bf16[1024,768]{1,0:T(8,128)(2,1)}) %all-gather.6.cloned.1.call-update) | async-done | bytes 1572880 | tf_op jit(solution)/shard_map/all_gather | solution.py:89
  467.4 4.6 fusion.9
  472.0 63.2 %all-gather.8.cloned.1.call-done = bf16[1024,768]{1,0:T(8,128)(2,1)} async-done(((bf16[128,768]{1,0:T(8,128)(2,1)}), bf16[1024,768]{1,0:T(8,128)(2,1)}) %all-gather.8.cloned.1.call-update) | async-done | bytes 1572880 | tf_op jit(solution)/shard_map/all_gather | solution.py:90
  535.2 3.9 add_convert_fusion
  540.6 4.3 all-to-all-start.6
  544.9 1.8 copy.84
  546.7 3.6 all_to_all.77
  550.3 13.2 %all-to-all-done.6 = bf16[32,32,640]{2,0,1:T(8,128)(2,1)} async-done(((bf16[32,32,640]{2,0,1:T(8,128)(2,1)}), bf16[32,32,640]{2,0,1:T(8,128)(2,1)}, u32[]{:S(2)}, u32[]{:S(2)}) %all-to-all-start.6) | async-done | bytes 1310752 | tf_op jit(solution)/shard_map/all_to_all | solution.py:110
  563.4 25.2 %all-to-all-start.5 = ((bf16[32,4,5120]{2,1,0:T(4,128)(2,1)}), bf16[32,4,5120]{2,1,0:T(4,128)(2,1)S(1)}, u32[]{:S(2)}, u32[]{:S(2)}) async-start(bf16[32,4,5120]{2,1,0:T(4,128)(2,1)} %all_to_all.77), calls=%async_computation.6 | async-start | bytes 2621440 | tf_op jit(solution)/shard_map/all_to_all | solution.py:100
  588.7 3.1 copy.94
  591.8 3.2 all_to_all.82
  595.0 3.4 copy.87
  598.4 22.0 %all-to-all-done.5 = bf16[32,4,5120]{2,1,0:T(4,128)(2,1)S(1)} async-done(((bf16[32,4,5120]{2,1,0:T(4,128)(2,1)}), bf16[32,4,5120]{2,1,0:T(4,128)(2,1)S(1)}, u32[]{:S(2)}, u32[]{:S(2)}) %all-to-all-start.5) | async-done | bytes 1310752 | tf_op jit(solution)/shard_map/all_to_all | solution.py:100
  621.5 5.7 all-to-all-start.7
  627.2 4.3 fusion.4
  631.5 2.2 fusion.2
  633.7 2.2 fusion.3
  635.9 2.5 reshape.51
  639.8 2.4 convolution_convert_fusion.1
  642.1 16.8 %all-to-all-done.7 = bf16[32,4,5120]{2,1,0:T(4,128)(2,1)} async-done(((bf16[32,4,5120]{2,1,0:T(4,128)(2,1)}), bf16[32,4,5120]{2,1,0:T(4,128)(2,1)}, u32[]{:S(2)}, u32[]{:S(2)}) %all-to-all-start.7) | async-done | bytes 1310752 | tf_op jit(solution)/shard_map/all_to_all | solution.py:109
  659.0 2.6 reshape.53
  661.5 1.7 convolution_convert_fusion
  (49 shorter events, 18.1 us)
Async XLA Ops:
  7.2 1.9 copy-start
  29.5 11.6 %copy-start.2 = (bf16[128,5120]{1,0:T(8,128)(2,1)S(1)}, bf16[128,5120]{1,0:T(8,128)(2,1)}, u32[]{:S(2)}) copy-start(bf16[128,5120]{1,0:T(8,128)(2,1)} %param.9) | copy-start | bytes 3932164
  29.5 36.8 %all-to-all-start.2 = ((bf16[8,2,40960]{2,1,0:T(2,128)(2,1)}), bf16[8,2,40960]{2,1,0:T(2,128)(2,1)}, u32[]{:S(2)}, u32[]{:S(2)}) async-start(bf16[8,2,40960]{2,1,0:T(2,128)(2,1)} %reshape.77), calls=%async_computation.2 | async-start | bytes 2621440 | tf_op jit(solution)/shard_map/all_to_all | solution.py:59
  66.3 27.3 %all-to-all-start = ((bf16[8,2,40960]{2,1,0:T(2,128)(2,1)}), bf16[8,2,40960]{2,1,0:T(2,128)(2,1)S(1)}, u32[]{:S(2)}, u32[]{:S(2)}) async-start(bf16[8,2,40960]{2,1,0:T(2,128)(2,1)} %reshape.79), calls=%async_computation | async-start | bytes 2621440 | tf_op jit(solution)/shard_map/all_to_all | solution.py:52
  93.6 54.9 %all-to-all-start.3 = ((bf16[32,32,640]{2,1,0:T(8,128)(2,1)}), bf16[32,32,640]{2,1,0:T(8,128)(2,1)}, u32[]{:S(2)}, u32[]{:S(2)}) async-start(bf16[32,32,640]{2,1,0:T(8,128)(2,1)} %copy.82), calls=%async_computation.3 | async-start | bytes 2621440 | tf_op jit(solution)/shard_map/all_to_all | solution.py:58
  148.5 37.4 %all-to-all-start.1 = ((bf16[32,32,640]{2,1,0:T(8,128)(2,1)}), bf16[32,32,640]{2,1,0:T(8,128)(2,1)S(1)}, u32[]{:S(2)}, u32[]{:S(2)}) async-start(bf16[32,32,640]{2,1,0:T(8,128)(2,1)} %copy.78), calls=%async_computation.1 | async-start | bytes 2621440 | tf_op jit(solution)/shard_map/all_to_all | solution.py:51
  154.1 163.9 %reduce-scatter.2.cloned.1.call-start = ((), (), s32[]{:S(2)}) async-start(), calls=%async_computation.9 | async-start | bytes 5308416 | tf_op jit(solution)/shard_map/reduce_scatter | solution.py:83
  185.9 3.1 copy-start.5
  185.9 3.1 copy-start.9
  189.0 1.4 copy-start.4
  192.8 191.5 %all-gather.4.cloned.1.call-start = ((), (), s32[]{:S(2)}) async-start(), calls=%async_computation.10 | async-start | bytes 1769472 | tf_op jit(solution)/shard_map/all_gather | solution.py:88
  320.2 147.2 %all-gather.6.cloned.1.call-start = ((), (), s32[]{:S(2)}) async-start(), calls=%async_computation.11 | async-start | bytes 1769472 | tf_op jit(solution)/shard_map/all_gather | solution.py:89
  320.9 214.3 %all-gather.8.cloned.1.call-start = ((), (), s32[]{:S(2)}) async-start(), calls=%async_computation.12 | async-start | bytes 1769472 | tf_op jit(solution)/shard_map/all_gather | solution.py:90
  388.8 151.8 %all-to-all-start.4 = ((bf16[32,32,640]{2,0,1:T(8,128)(2,1)}), bf16[32,32,640]{2,0,1:T(8,128)(2,1)S(1)}, u32[]{:S(2)}, u32[]{:S(2)}) async-start(bf16[32,32,640]{2,0,1:T(8,128)(2,1)} %copy.83), calls=%async_computation.5 | async-start | bytes 2621440 | tf_op jit(solution)/shard_map/all_to_all | solution.py:101
  540.6 22.8 %all-to-all-start.6 = ((bf16[32,32,640]{2,0,1:T(8,128)(2,1)}), bf16[32,32,640]{2,0,1:T(8,128)(2,1)}, u32[]{:S(2)}, u32[]{:S(2)}) async-start(bf16[32,32,640]{2,0,1:T(8,128)(2,1)} %copy.85), calls=%async_computation.7 | async-start | bytes 2621440 | tf_op jit(solution)/shard_map/all_to_all | solution.py:110
  563.4 57.0 %all-to-all-start.5 = ((bf16[32,4,5120]{2,1,0:T(4,128)(2,1)}), bf16[32,4,5120]{2,1,0:T(4,128)(2,1)S(1)}, u32[]{:S(2)}, u32[]{:S(2)}) async-start(bf16[32,4,5120]{2,1,0:T(4,128)(2,1)} %all_to_all.77), calls=%async_computation.6 | async-start | bytes 2621440 | tf_op jit(solution)/shard_map/all_to_all | solution.py:100
  620.4 1.1 copy-start.3
  621.5 37.5 %all-to-all-start.7 = ((bf16[32,4,5120]{2,1,0:T(4,128)(2,1)}), bf16[32,4,5120]{2,1,0:T(4,128)(2,1)}, u32[]{:S(2)}, u32[]{:S(2)}) async-start(bf16[32,4,5120]{2,1,0:T(4,128)(2,1)} %copy.87), calls=%async_computation.8 | async-start | bytes 2621440 | tf_op jit(solution)/shard_map/all_to_all | solution.py:109
  627.2 4.3 copy-start.6
  627.2 4.3 copy-start.7
  631.5 2.2 copy-start.8
  659.0 4.2 copy-start.1
Sparse Core Ops, SparseCore 0:
  192.9 125.0 reduce-scatter.1
  321.2 63.0 all-gather.3
  387.5 79.8 all-gather.5
  470.4 64.7 all-gather.7
where the time goes:
time: 672 us; the launch traced here: 670 us
  waiting for transfers between devices  432 us (64%)
  local copies, waits for them, and re-layouts  97.9 us (15%)
  starting transfers between devices  86 us (13%)
  matrix products  33 us (5%)
  between operations  14 us (2%)
  other arithmetic  6.97 us (1%)
    reduce_scatter x1, waiting for transfers between devices, body(): lax.psum_scatter(terms.astype(jnp.bfloat16), 'dp', scatter_dimension=0, t...  125 us
    all_gather x1, waiting for transfers between devices, body(): lax.all_gather(own_grad_gate, 'dp', axis=0, tiled=True)  74.9 us
    all_gather x1, waiting for transfers between devices, body(): lax.all_gather(own_grad_up, 'dp', axis=0, tiled=True)  63.2 us
    all_gather x1, waiting for transfers between devices, body(): lax.all_gather(own_hidden, 'dp', axis=0, tiled=True)  62.8 us
    unnamed x27, local copies, waits for them, and re-layouts  33.2 us
    all_to_all x1, waiting for transfers between devices, body(): lax.all_to_all(lax.all_to_all(outgoing[0], 'dp', split_axis=2, concat_axi...  27.5 us
    all_to_all x1, starting transfers between devices, body(): lax.all_to_all(lax.all_to_all(expert_out.reshape(arrived_shape), 'dp', sp...  25.2 us
    all_to_all x1, starting transfers between devices, body(): lax.all_to_all(lax.all_to_all(outgoing[1], 'dp', split_axis=2, concat_axi...  23.1 us
  transfers between devices with their start and end apart: 12, of which 11 were waited for; matrix products, arithmetic and copies ran while one was open for 14% of the time, Pallas kernels for 0%

commit v1 on v0

v1 whole, which is shorter than its diff:
```python
import functools

import jax
import jax.numpy as jnp
from jax import lax
from jax.experimental import pallas as pl
from jax.experimental.pallas import tpu as pltpu
from jax.sharding import PartitionSpec as P

MESH = pl.DeviceIdType.MESH
F32 = jnp.float32
BF16 = jnp.bfloat16


def nn(a, b):
    return lax.dot_general(a, b, (((1,), (0,)), ((), ())), preferred_element_type=F32)


def nt(a, b):
    return lax.dot_general(a, b, (((1,), (1,)), ((), ())), preferred_element_type=F32)


def tn(a, b):
    return lax.dot_general(a, b, (((0,), (0,)), ((), ())), preferred_element_type=F32)


def select_rows(rows, cols, shift):
    i = lax.broadcasted_iota(jnp.int32, (rows, cols), 0)
    c = lax.broadcasted_iota(jnp.int32, (rows, cols), 1)
    want = (i // 4) * 8 + i % 4 + shift
    return (want == c).astype(BF16)


def place_rows(rows, cols, shift):
    i = lax.broadcasted_iota(jnp.int32, (rows, cols), 1)
    c = lax.broadcasted_iota(jnp.int32, (rows, cols), 0)
    want = (i // 4) * 8 + i % 4 + shift
    return (want == c).astype(BF16)


def kernel(
    geo,
    tok, cot, idx_col, scale_col, idx_row, gate_row, wg, wu, wd,
    mixed, tgrad, ggrad, gwg, gwu, gwd,
    sbuf, rbuf, xs, ys, terms, s1, t1, s2, s3, zb_out, fin, ag, bbuf,
    a2a_send, a2a_recv, rs_send, rs_recv, z_send, z_recv, ag_send, ag_recv,
    az_send, az_recv, cb_send, cb_recv,
):
    nx, nzh, nzl, ny, nc = geo
    ne = nzl * ny * nc
    nb = nx * nzh
    n = nb * ne
    rows = ne * 8
    half = ne * 4
    tdev = tok.shape[0]
    wide = wg.shape[0]
    ff = wg.shape[1]
    hw = 3 * ff // 2
    hf = ff // 2
    dp = lax.axis_index("dp")
    ex = lax.axis_index("expert")
    me = dp * ne + ex
    x, zh = lax.div(dp, nzh), lax.rem(dp, nzh)
    core = lax.rem(ex, nc)
    yy = lax.rem(lax.div(ex, nc), ny)
    zl = lax.div(ex, nc * ny)
    zz = zh * nzl + zl

    def partner(i):
        o = lax.rem(i * 97, n)
        dc, r = lax.rem(o, nc), lax.div(o, nc)
        dx, r = lax.rem(r, nx), lax.div(r, nx)
        dy, dz = lax.rem(r, ny), lax.div(r, ny)
        px = lax.rem(x + dx, nx)
        py = lax.rem(yy + dy, ny)
        pz = lax.rem(zz + dz, nzh * nzl)
        pc = lax.rem(core + dc, nc)
        pdp = px * nzh + lax.div(pz, nzl)
        pex = (lax.rem(pz, nzl) * ny + py) * nc + pc
        return pdp, pex

    barrier = pltpu.get_barrier_semaphore()

    def greet(i, carry):
        pdp, pex = partner(i)
        pl.semaphore_signal(barrier, inc=1, device_id=(pdp, pex), device_id_type=MESH)
        return carry

    lax.fori_loop(1, n, greet, 0)

    lane = lax.broadcasted_iota(jnp.int32, (rows, tdev), 1)
    ids = idx_col[...]
    hot_t = (lane == ids).astype(BF16)
    hot_c = (lane + tdev == ids).astype(BF16)

    def gather(k, carry):
        at = pl.ds(pl.multiple_of(k * wide, 128), wide)
        got = nn(hot_t, tok[:, at]) + nn(hot_c, cot[:, at])
        got = got * scale_col[...]
        sbuf[pl.ds(k * ne, ne)] = got.reshape(ne, 8, wide).astype(BF16)
        return carry

    lax.fori_loop(0, nb, gather, 0)
    pl.semaphore_wait(barrier, n - 1)

    def exchange(src, dst, send_sem, recv_sem):
        def send(i, carry):
            pdp, pex = partner(i)
            pltpu.make_async_remote_copy(
                src_ref=src.at[pdp * ne + pex],
                dst_ref=dst.at[me],
                send_sem=send_sem,
                recv_sem=recv_sem,
                device_id=(pdp, pex),
                device_id_type=MESH,
            ).start()
            return carry

        lax.fori_loop(1, n, send, 0)
        pltpu.make_async_copy(src.at[me], dst.at[me], recv_sem).start()

    def arrived(dst, recv_sem):
        pltpu.make_async_copy(dst, dst, recv_sem).wait()

    def sent(src, send_sem):
        part = src.at[pl.ds(0, n - 1)]
        pltpu.make_async_copy(part, part, send_sem).wait()

    exchange(sbuf, rbuf, a2a_send, a2a_recv)
    arrived(rbuf, a2a_recv)

    pick_x = select_rows(half, rows, 0)
    pick_y = select_rows(half, rows, 4)

    def products(b, carry):
        z = rbuf[pl.ds(b * ne, ne)].reshape(rows, wide)
        xb = nn(pick_x, z).astype(BF16)
        yb = nn(pick_y, z).astype(BF16)
        xs[b] = xb
        ys[b] = yb
        terms[b, 0, :, :ff] = nn(xb, wg[...]).astype(BF16)
        up = nn(xb, wu[...]).astype(BF16)
        terms[b, 0, :, ff:] = up[:, :hf]
        terms[b, 1, :, :hf] = up[:, hf:]
        terms[b, 1, :, hf:] = nt(yb, wd[...]).astype(BF16)
        return carry

    lax.fori_loop(0, nb, products, 0)

    to = (lax.rem(x + 1, nx), lax.rem(x + nx - 1, nx))
    come = (to[1], to[0])
    opposite = lax.rem(x + 2, nx)
    side = (1 - zh, zh)

    def blk(q, s):
        return q * nzh + s

    def remote(src, dst, send_sem, recv_sem, pdp):
        copy = pltpu.make_async_remote_copy(
            src_ref=src, dst_ref=dst, send_sem=send_sem, recv_sem=recv_sem,
            device_id=(pdp, ex), device_id_type=MESH,
        )
        copy.start()
        return copy

    def wait_for(dst, sem):
        pltpu.make_async_copy(dst, dst, sem).wait()

    sends = []

    def rs_first(c):
        for h in (0, 1):
            sends.append(remote(terms.at[blk(opposite, side[c]), h], s1.at[c, h, 1],
                                rs_send.at[c, h, 0], rs_recv.at[c, h, 0], blk(to[h], zh)))
        for h in (0, 1):
            sends.append(remote(terms.at[blk(to[h], side[c]), 1 - h], s1.at[c, 1 - h, 0],
                                rs_send.at[c, h, 1], rs_recv.at[c, 1 - h, 1], blk(to[h], zh)))

    def rs_pass(c):
        for h in (0, 1):
            wait_for(s1.at[c, h, 1], rs_recv.at[c, h, 0])
            t1[c, h] = (terms[blk(to[h], side[c]), h].astype(F32) + s1[c, h, 1].astype(F32)).astype(BF16)
            sends.append(remote(t1.at[c, h], s2.at[c, h], rs_send.at[c, h, 2], rs_recv.at[c, h, 2],
                                blk(to[h], zh)))

    def rs_total(c, h):
        wait_for(s1.at[c, h, 0], rs_recv.at[c, h, 1])
        wait_for(s2.at[c, h], rs_recv.at[c, h, 2])
        return (terms[blk(x, side[c]), h].astype(F32) + s1[c, h, 0].astype(F32)
                + s2[c, h].astype(F32))

    zpeer = blk(x, 1 - zh)
    rs_first(0)
    rs_pass(0)
    rs_first(1)
    for h in (0, 1):
        zb_out[h] = rs_total(0, h).astype(BF16)
        sends.append(remote(zb_out.at[h], s3.at[h], z_send.at[h], z_recv.at[h], zpeer))
    rs_pass(1)
    for h in (0, 1):
        fin[h] = rs_total(1, h)
    for h in (0, 1):
        wait_for(s3.at[h], z_recv.at[h])

    step = half // 4

    def activate(i, carry):
        at = pl.ds(pl.multiple_of(i * step, step), step)
        lo = fin[0, at, :] + s3[0, at, :].astype(F32)
        hi = fin[1, at, :] + s3[1, at, :].astype(F32)
        gate = lo[:, :ff]
        up = jnp.concatenate([lo[:, ff:], hi[:, :hf]], axis=1)
        back = hi[:, hf:]
        sig = 1.0 / (1.0 + jnp.exp(-gate))
        silu = gate * sig
        hidden = (silu * up).astype(BF16)
        g_up = (back * silu).astype(BF16)
        g_gate = (back * up * sig * (1.0 + gate * (1.0 - sig))).astype(BF16)
        ag[dp, 0, at, :ff] = hidden
        ag[dp, 0, at, ff:] = g_gate[:, :hf]
        ag[dp, 1, at, :hf] = g_gate[:, hf:]
        ag[dp, 1, at, hf:] = g_up
        return carry

    lax.fori_loop(0, 4, activate, 0)

    for h in (0, 1):
        sends.append(remote(ag.at[dp, h], ag.at[dp, h], az_send.at[h], az_recv.at[h], zpeer))

    def ag_first(c, s):
        mine = blk(x, s)
        for j in (0, 1):
            for h in (0, 1):
                g = h if j == 0 else 1 - h
                sends.append(remote(ag.at[mine, g], ag.at[mine, g], ag_send.at[c, h, j],
                                    ag_recv.at[c, h, j], blk(to[h], zh)))

    def ag_pass(c, s):
        for h in (0, 1):
            got = blk(come[h], s)
            wait_for(ag.at[got, h], ag_recv.at[c, h, 0])
            sends.append(remote(ag.at[got, h], ag.at[got, h], ag_send.at[c, h, 2],
                                ag_recv.at[c, h, 2], blk(to[h], zh)))

    def ag_rest(c, s):
        for h in (0, 1):
            wait_for(ag.at[blk(come[h], s), 1 - h], ag_recv.at[c, h, 1])
            wait_for(ag.at[blk(opposite, s), h], ag_recv.at[c, h, 2])

    ag_first(0, zh)
    ag_pass(0, zh)
    for h in (0, 1):
        wait_for(ag.at[zpeer, h], az_recv.at[h])
    ag_first(1, 1 - zh)
    ag_pass(1, 1 - zh)
    ag_rest(0, zh)
    ag_rest(1, 1 - zh)

    sent(sbuf, a2a_send)
    put_x = place_rows(rows, half, 0)
    put_y = place_rows(rows, half, 4)

    def outputs(b, carry):
        out = nn(ag[b, 0, :, :ff], wd[...]).astype(BF16)
        grad = nt(ag[b, 0, :, ff:], wg[:, :hf]) + nt(ag[b, 1, :, :hf], wg[:, hf:])
        grad = (grad + nt(ag[b, 1, :, hf:], wu[...])).astype(BF16)
        both = nn(put_x, out) + nn(put_y, grad)
        sbuf[pl.ds(b * ne, ne)] = both.reshape(ne, 8, wide).astype(BF16)
        return carry

    lax.fori_loop(0, nb, outputs, 0)
    exchange(sbuf, bbuf, cb_send, cb_recv)

    all_rows = nb * half

    def grads_in(m, carry):
        at = pl.ds(pl.multiple_of(m * 128, 128), 128)
        xt = xs[:, :, at].reshape(all_rows, 128)
        gwg[at, :hf] = tn(xt, ag[:, 0, :, ff:].reshape(all_rows, hf)).astype(BF16)
        rest = tn(xt, ag[:, 1, :, :].reshape(all_rows, hw))
        gwg[at, hf:] = rest[:, :hf].astype(BF16)
        gwu[at, :] = rest[:, hf:].astype(BF16)
        return carry

    lax.fori_loop(0, wide // 128, grads_in, 0)

    def grads_down(m, carry):
        at = pl.ds(pl.multiple_of(m * 128, 128), 128)
        ht = ag[:, 0, :, at].reshape(all_rows, 128)
        gwd[at, :] = tn(ht, ys[...].reshape(all_rows, wide)).astype(BF16)
        return carry

    lax.fori_loop(0, ff // 128, grads_down, 0)

    arrived(bbuf, cb_recv)
    tline = lax.broadcasted_iota(jnp.int32, (tdev, rows), 0)
    to_out = tline == idx_row[...]
    to_grad = (tline + tdev == idx_row[...]).astype(BF16)
    weight = jnp.where(to_out, gate_row[...], 0.0)
    w_hi = weight.astype(BF16)
    w_lo = (weight - w_hi.astype(F32)).astype(BF16)

    def combine(k, prods):
        at = pl.ds(pl.multiple_of(k * wide, 128), wide)
        z = bbuf[pl.ds(k * ne, ne)].reshape(rows, wide)
        mixed[:, at] = (nn(w_hi, z) + nn(w_lo, z)).astype(BF16)
        tgrad[:, at] = nn(to_grad, z).astype(BF16)
        return prods + nt(z, cot[:, at])

    prods = lax.fori_loop(0, nb, combine, jnp.zeros((rows, tdev), F32))
    ggrad[...] = jnp.sum(jnp.where(lane == ids, prods, 0.0), axis=1, keepdims=True)
    for copy in sends:
        copy.wait_send()
    sent(sbuf, cb_send)


def body(geo, tokens, cotangent, picks, gates, w_gate, w_up, w_down):
    nx, nzh, nzl, ny, nc = geo
    ne, slots = picks.shape[1], picks.shape[2]
    nb = nx * nzh
    n = nb * ne
    tdev, model = tokens.shape
    wide, ff = w_gate.shape[1], w_gate.shape[2]
    rows, half, hw = ne * 8, ne * 4, 3 * ff // 2
    chosen, scale = picks[0], gates[0]
    idx = jnp.concatenate([chosen, chosen + tdev], axis=1)
    weight = jnp.concatenate([jnp.ones_like(scale), scale], axis=1)
    gate = jnp.concatenate([scale, scale], axis=1)
    vm = pl.BlockSpec(memory_space=pltpu.VMEM)
    outs = pl.pallas_call(
        functools.partial(kernel, geo),
        out_shape=(
            jax.ShapeDtypeStruct((tdev, model), BF16),
            jax.ShapeDtypeStruct((tdev, model), BF16),
            jax.ShapeDtypeStruct((rows, 1), F32),
            jax.ShapeDtypeStruct((wide, ff), BF16),
            jax.ShapeDtypeStruct((wide, ff), BF16),
            jax.ShapeDtypeStruct((ff, wide), BF16),
        ),
        in_specs=[vm] * 9,
        out_specs=(vm,) * 6,
        scratch_shapes=[
            pltpu.VMEM((n, 8, wide), BF16),
            pltpu.VMEM((n, 8, wide), BF16),
            pltpu.VMEM((nb, half, wide), BF16),
            pltpu.VMEM((nb, half, wide), BF16),
            pltpu.VMEM((nb, 2, half, hw), BF16),
            pltpu.VMEM((2, 2, 2, half, hw), BF16),
            pltpu.VMEM((2, 2, half, hw), BF16),
            pltpu.VMEM((2, 2, half, hw), BF16),
            pltpu.VMEM((2, half, hw), BF16),
            pltpu.VMEM((2, half, hw), BF16),
            pltpu.VMEM((2, half, hw), F32),
            pltpu.VMEM((nb, 2, half, hw), BF16),
            pltpu.VMEM((n, 8, wide), BF16),
            pltpu.SemaphoreType.DMA,
            pltpu.SemaphoreType.DMA,
            pltpu.SemaphoreType.DMA((2, 2, 3)),
            pltpu.SemaphoreType.DMA((2, 2, 3)),
            pltpu.SemaphoreType.DMA((2,)),
            pltpu.SemaphoreType.DMA((2,)),
            pltpu.SemaphoreType.DMA((2, 2, 3)),
            pltpu.SemaphoreType.DMA((2, 2, 3)),
            pltpu.SemaphoreType.DMA((2,)),
            pltpu.SemaphoreType.DMA((2,)),
            pltpu.SemaphoreType.DMA,
            pltpu.SemaphoreType.DMA,
        ],
        compiler_params=pltpu.CompilerParams(
            collective_id=0, has_side_effects=True, vmem_limit_bytes=62 * 1024 * 1024
        ),
        name="moe",
    )(
        tokens, cotangent, idx.reshape(rows, 1), weight.reshape(rows, 1),
        idx.reshape(1, rows), gate.reshape(1, rows), w_gate[0], w_up[0], w_down[0],
    )
    mixed, tgrad, ggrad, gwg, gwu, gwd = outs
    gate_grad = ggrad.reshape(ne, 8)[:, :slots].reshape(1, ne, slots)
    return (mixed, tgrad, gate_grad, gwg[None], gwu[None], gwd[None])


def solution(mesh):
    ne = mesh.shape["expert"]
    geo = (4, 2, 4, 4, 2) if ne == 32 else (4, 2, 1, 1, ne)
    return jax.shard_map(
        functools.partial(body, geo),
        mesh=mesh,
        in_specs=(
            P(("dp", "expert"), None),
            P(("dp", "expert"), None),
            P(("dp", "expert"), None, None),
            P(("dp", "expert"), None, None),
            P("expert", "dp", None),
            P("expert", "dp", None),
            P("expert", None, "dp"),
        ),
        out_specs=(
            P(("dp", "expert"), None),
            P(("dp", "expert"), None),
            P(("dp", "expert"), None, None),
            P("expert", "dp", None),
            P("expert", "dp", None),
            P("expert", None, "dp"),
        ),
        check_vma=False,
    )
```

time: 672 us -> 283 us (0.42)
  waiting for transfers between devices: 432 us -> 0 us
  Pallas kernels: 0 us -> 265 us
  starting transfers between devices: 86 us -> 0 us
  local copies, waits for them, and re-layouts: 97.9 us -> 12.9 us
  matrix products: 33 us -> 0 us
  between operations: 14 us -> 0.66 us
    pallas_call x0 -> x1, Pallas kernels: none -> 265 us  [body(): pl.pallas_call(functools.partial(kernel, geo), out_shape=(jax.ShapeDtypeS...]
    all_gather x3 -> x0, waiting for transfers between devices: 201 us -> none  [the longest x1 74.9 us: body(): lax.all_gather(own_grad_gate, 'dp', axis=0, tiled=True)]
    reduce_scatter x1 -> x0, waiting for transfers between devices: 125 us -> none  [body(): lax.psum_scatter(terms.astype(jnp.bfloat16), 'dp', scatter_dimension=0, t...]
    all_to_all x8 -> x0, waiting for transfers between devices: 105 us -> none  [the longest x1 27.5 us: body(): lax.all_to_all(lax.all_to_all(outgoing[0], 'dp', split_axis=2, concat_axi...]
    all_to_all x8 -> x0, starting transfers between devices: 85.6 us -> none  [the longest x1 25.2 us: body(): lax.all_to_all(lax.all_to_all(expert_out.reshape(arrived_shape), 'dp', sp...]
    dot_general x11 -> x0, matrix products: 33 us -> none  [the longest x3 12.7 us: contract_cols(): lax.dot_general(left, right, (((1,), (1,)), ((), ())), preferred_element_...]
    all_to_all x9 -> x0, local copies, waits for them, and re-layouts: 32.5 us -> none  [the longest x2 9.89 us: body(): lax.all_to_all(outgoing[1], 'dp', split_axis=2, concat_axis=1, tiled=True)]
    reshape x9 -> x5, local copies, waits for them, and re-layouts: 28.3 us -> 2.89 us  [the longest x1 0.76 us: body(): weight.reshape(rows, 1)]
  transfers between devices with their start and end apart: 12 -> 0, of which waited for: 11 -> 0; matrix products, arithmetic and copies ran while one was open for 14% -> 0% of each run, Pallas kernels for 0% -> 0%
where the time goes in v1:
time: 283 us; the launch traced here: 281 us
  Pallas kernels  265 us (94%)
  local copies, waits for them, and re-layouts  12.9 us (5%)
  other arithmetic  3.15 us (1%)
    pallas_call x1, Pallas kernels, body(): pl.pallas_call(functools.partial(kernel, geo), out_shape=(jax.ShapeDtypeS...  265 us
    unnamed x14, local copies, waits for them, and re-layouts  9.05 us

profile of v1, /device:TPU:1, one launch (start us, length us, event | category | flops | bytes accessed | tf_op | source)
XLA Modules:
  0.0 281.3 jit_solution(1246598034420059478)
XLA Ops:
  0.6 0.7 broadcast_add_fusion
  1.3 0.7 pad_add_fusion
  2.0 0.8 pad_maximum_fusion
  2.8 0.1 copy.18
  2.8 0.7 reshape.32.idx_row
  3.5 0.1 copy.21
  3.6 0.7 reshape.33.gate_row
  4.2 0.8 copy.25
  5.0 0.1 concatenate.10.clone
  5.1 0.8 reshape.37.scale_col
  5.8 0.8 reshape.36.idx_col
  6.6 264.6 %moe.1 = (bf16[128,5120]{1,0:T(8,128)(2,1)}, bf16[128,5120]{1,0:T(8,128)(2,1)}, f32[256,1]{1,0:T(8,128)}, bf16[640,768]{1,0:T(8,128)(2,1)}, bf16[640,768]{1,0:T(8,128)(2,1)}, /*index=5*/bf16[768,640]{1,0:T(8,128)(2,1)}) custom-call(bf16[128,5120]{1,0:T(8,128)(2,1)} %tok.1, bf16[128,5120]{1,0:T(8,128)(2,1)} %cot.1, s32[256,1]{1,0:T(8,128)} %reshape.36.idx_col, ...), custom_call_target="tpu_custom_call" | custom-call | tf_op jit(solution)/shard_map/moe/pallas_call | solution.py:330
  271.2 1.0 reduce
  272.2 0.1 reshape.34
  272.3 0.7 copy.24
  273.0 0.0 copy-start
  273.0 2.6 copy.31
  275.5 0.0 copy-done
  275.5 0.0 copy-start.3
  275.5 1.1 copy.32
  276.6 0.6 copy-done.3
  277.2 0.0 copy-start.2
  277.2 0.9 copy.33
  278.2 0.6 copy-done.2
  278.8 0.0 copy-start.1
  278.8 0.9 copy.34
  279.7 0.6 copy-done.1
  280.3 0.9 copy.35
Async XLA Ops:
  273.0 2.6 copy-start
  275.5 1.7 copy-start.3
  277.2 1.6 copy-start.2
  278.8 1.6 copy-start.1

commit v2 on v1

--- a/solution.py
+++ b/solution.py
@@ -10,6 +10,7 @@
 MESH = pl.DeviceIdType.MESH
 F32 = jnp.float32
 BF16 = jnp.bfloat16
+GREET = 5
 
 
 def nn(a, b):
@@ -40,7 +41,7 @@
 
 def kernel(
     geo,
-    tok, cot, idx_col, scale_col, idx_row, gate_row, wg, wu, wd,
+    tok, cot, pick_row, gate_row, wg, wu, wd,
     mixed, tgrad, ggrad, gwg, gwu, gwd,
     sbuf, rbuf, xs, ys, terms, s1, t1, s2, s3, zb_out, fin, ag, bbuf,
     a2a_send, a2a_recv, rs_send, rs_recv, z_send, z_recv, ag_send, ag_recv,
@@ -50,6 +51,8 @@
     ne = nzl * ny * nc
     nb = nx * nzh
     n = nb * ne
+    nz = nzh * nzl
+    per = nz * ny * nc
     rows = ne * 8
     half = ne * 4
     tdev = tok.shape[0]
@@ -66,73 +69,69 @@
     zl = lax.div(ex, nc * ny)
     zz = zh * nzl + zl
 
-    def partner(i):
-        o = lax.rem(i * 97, n)
-        dc, r = lax.rem(o, nc), lax.div(o, nc)
-        dx, r = lax.rem(r, nx), lax.div(r, nx)
-        dy, dz = lax.rem(r, ny), lax.div(r, ny)
-        px = lax.rem(x + dx, nx)
-        py = lax.rem(yy + dy, ny)
-        pz = lax.rem(zz + dz, nzh * nzl)
-        pc = lax.rem(core + dc, nc)
-        pdp = px * nzh + lax.div(pz, nzl)
-        pex = (lax.rem(pz, nzl) * ny + py) * nc + pc
-        return pdp, pex
-
     barrier = pltpu.get_barrier_semaphore()
 
     def greet(i, carry):
-        pdp, pex = partner(i)
-        pl.semaphore_signal(barrier, inc=1, device_id=(pdp, pex), device_id_type=MESH)
+        other = lax.rem(me + i, n)
+        pl.semaphore_signal(barrier, inc=1, device_id=other, device_id_type=pl.DeviceIdType.LOGICAL)
         return carry
 
-    lax.fori_loop(1, n, greet, 0)
-
-    lane = lax.broadcasted_iota(jnp.int32, (rows, tdev), 1)
-    ids = idx_col[...]
-    hot_t = (lane == ids).astype(BF16)
-    hot_c = (lane + tdev == ids).astype(BF16)
+    lax.fori_loop(1, n, greet, 0, unroll=GREET)
+
+    pick_x = select_rows(half, rows, 0)
+    pick_y = select_rows(half, rows, 4)
+    put_x = place_rows(rows, half, 0)
+    put_y = place_rows(rows, half, 4)
+    eye = lax.broadcasted_iota(jnp.int32, (half, half), 0) == lax.broadcasted_iota(
+        jnp.int32, (half, half), 1
+    )
+    pick_col = jnp.sum(jnp.where(eye, pick_row[...], 0), axis=1, keepdims=True)
+    gate_col = jnp.sum(jnp.where(eye, gate_row[...], 0.0), axis=1, keepdims=True)
+    hot = (lax.broadcasted_iota(jnp.int32, (half, tdev), 1) == pick_col).astype(BF16)
 
     def gather(k, carry):
         at = pl.ds(pl.multiple_of(k * wide, 128), wide)
-        got = nn(hot_t, tok[:, at]) + nn(hot_c, cot[:, at])
-        got = got * scale_col[...]
-        sbuf[pl.ds(k * ne, ne)] = got.reshape(ne, 8, wide).astype(BF16)
+        token_rows = nn(hot, tok[:, at]).astype(BF16)
+        grad_rows = (nn(hot, cot[:, at]) * gate_col).astype(BF16)
+        both = nn(put_x, token_rows) + nn(put_y, grad_rows)
+        sbuf[pl.ds(k * ne, ne)] = both.reshape(ne, 8, wide).astype(BF16)
         return carry
 
     lax.fori_loop(0, nb, gather, 0)
     pl.semaphore_wait(barrier, n - 1)
 
-    def exchange(src, dst, send_sem, recv_sem):
+    def dispatch(ways, first):
         def send(i, carry):
-            pdp, pex = partner(i)
+            dx = ways[0]
+            if len(ways) == 2:
+                dx = ways[0] + (ways[1] - ways[0]) * lax.rem(i, 2)
+            o = lax.rem(lax.div(i, len(ways)) * 37, per)
+            dc, r = lax.rem(o, nc), lax.div(o, nc)
+            dz, dy = lax.rem(r, nz), lax.div(r, nz)
+            pz = lax.rem(zz + dz, nz)
+            pdp = lax.rem(x + dx, nx) * nzh + lax.div(pz, nzl)
+            pex = (lax.rem(pz, nzl) * ny + lax.rem(yy + dy, ny)) * nc + lax.rem(core + dc, nc)
             pltpu.make_async_remote_copy(
-                src_ref=src.at[pdp * ne + pex],
-                dst_ref=dst.at[me],
-                send_sem=send_sem,
-                recv_sem=recv_sem,
-                device_id=(pdp, pex),
-                device_id_type=MESH,
+                src_ref=sbuf.at[pdp * ne + pex], dst_ref=rbuf.at[me],
+                send_sem=a2a_send, recv_sem=a2a_recv.at[dp],
+                device_id=(pdp, pex), device_id_type=MESH,
             ).start()
             return carry
 
-        lax.fori_loop(1, n, send, 0)
-        pltpu.make_async_copy(src.at[me], dst.at[me], recv_sem).start()
-
-    def arrived(dst, recv_sem):
-        pltpu.make_async_copy(dst, dst, recv_sem).wait()
+        lax.fori_loop(first, per * len(ways), send, 0)
+
+    dispatch((2,), 0)
+    dispatch((1, 3), 0)
+    dispatch((0,), 1)
+    pltpu.make_async_copy(sbuf.at[me], rbuf.at[me], a2a_recv.at[dp]).start()
 
     def sent(src, send_sem):
         part = src.at[pl.ds(0, n - 1)]
         pltpu.make_async_copy(part, part, send_sem).wait()
 
-    exchange(sbuf, rbuf, a2a_send, a2a_recv)
-    arrived(rbuf, a2a_recv)
-
-    pick_x = select_rows(half, rows, 0)
-    pick_y = select_rows(half, rows, 4)
-
-    def products(b, carry):
+    def products(b):
+        part = rbuf.at[pl.ds(b * ne, ne)]
+        pltpu.make_async_copy(part, part, a2a_recv.at[b]).wait()
         z = rbuf[pl.ds(b * ne, ne)].reshape(rows, wide)
         xb = nn(pick_x, z).astype(BF16)
         yb = nn(pick_y, z).astype(BF16)
@@ -143,9 +142,6 @@
         terms[b, 0, :, ff:] = up[:, :hf]
         terms[b, 1, :, :hf] = up[:, hf:]
         terms[b, 1, :, hf:] = nt(yb, wd[...]).astype(BF16)
-        return carry
-
-    lax.fori_loop(0, nb, products, 0)
 
     to = (lax.rem(x + 1, nx), lax.rem(x + nx - 1, nx))
     come = (to[1], to[0])
@@ -172,11 +168,11 @@
         for h in (0, 1):
             sends.append(remote(terms.at[blk(opposite, side[c]), h], s1.at[c, h, 1],
                                 rs_send.at[c, h, 0], rs_recv.at[c, h, 0], blk(to[h], zh)))
+
+    def rs_pass(c):
         for h in (0, 1):
             sends.append(remote(terms.at[blk(to[h], side[c]), 1 - h], s1.at[c, 1 - h, 0],
                                 rs_send.at[c, h, 1], rs_recv.at[c, 1 - h, 1], blk(to[h], zh)))
-
-    def rs_pass(c):
         for h in (0, 1):
             wait_for(s1.at[c, h, 1], rs_recv.at[c, h, 0])
             t1[c, h] = (terms[blk(to[h], side[c]), h].astype(F32) + s1[c, h, 1].astype(F32)).astype(BF16)
@@ -189,16 +185,27 @@
         return (terms[blk(x, side[c]), h].astype(F32) + s1[c, h, 0].astype(F32)
                 + s2[c, h].astype(F32))
 
+    def products_of(first, gap, count):
+        def one(i, carry):
+            products(blk(lax.rem(first + gap * lax.div(i, nzh), nx), lax.rem(i, nzh)))
+            return carry
+
+        lax.fori_loop(0, count * nzh, one, 0)
+
     zpeer = blk(x, 1 - zh)
+    products_of(opposite, 0, 1)
     rs_first(0)
+    rs_first(1)
+    products_of(x + 1, 2, 2)
     rs_pass(0)
-    rs_first(1)
+    rs_pass(1)
+    products_of(x, 0, 1)
     for h in (0, 1):
         zb_out[h] = rs_total(0, h).astype(BF16)
         sends.append(remote(zb_out.at[h], s3.at[h], z_send.at[h], z_recv.at[h], zpeer))
-    rs_pass(1)
     for h in (0, 1):
         fin[h] = rs_total(1, h)
+    sent(sbuf, a2a_send)
     for h in (0, 1):
         wait_for(s3.at[h], z_recv.at[h])
 
@@ -224,16 +231,12 @@
 
     lax.fori_loop(0, 4, activate, 0)
 
-    for h in (0, 1):
-        sends.append(remote(ag.at[dp, h], ag.at[dp, h], az_send.at[h], az_recv.at[h], zpeer))
-
-    def ag_first(c, s):
+    def ag_first(c, s, g):
         mine = blk(x, s)
-        for j in (0, 1):
-            for h in (0, 1):
-                g = h if j == 0 else 1 - h
-                sends.append(remote(ag.at[mine, g], ag.at[mine, g], ag_send.at[c, h, j],
-                                    ag_recv.at[c, h, j], blk(to[h], zh)))
+        for h in (g, 1 - g):
+            j = 0 if g == h else 1
+            sends.append(remote(ag.at[mine, g], ag.at[mine, g], ag_send.at[c, h, j],
+                                ag_recv.at[c, h, j], blk(to[h], zh)))
 
     def ag_pass(c, s):
         for h in (0, 1):
@@ -242,34 +245,63 @@
             sends.append(remote(ag.at[got, h], ag.at[got, h], ag_send.at[c, h, 2],
                                 ag_recv.at[c, h, 2], blk(to[h], zh)))
 
-    def ag_rest(c, s):
-        for h in (0, 1):
-            wait_for(ag.at[blk(come[h], s), 1 - h], ag_recv.at[c, h, 1])
-            wait_for(ag.at[blk(opposite, s), h], ag_recv.at[c, h, 2])
-
-    ag_first(0, zh)
-    ag_pass(0, zh)
-    for h in (0, 1):
-        wait_for(ag.at[zpeer, h], az_recv.at[h])
-    ag_first(1, 1 - zh)
-    ag_pass(1, 1 - zh)
-    ag_rest(0, zh)
-    ag_rest(1, 1 - zh)
-
-    sent(sbuf, a2a_send)
-    put_x = place_rows(rows, half, 0)
-    put_y = place_rows(rows, half, 4)
-
-    def outputs(b, carry):
+    def outputs(b, first):
         out = nn(ag[b, 0, :, :ff], wd[...]).astype(BF16)
         grad = nt(ag[b, 0, :, ff:], wg[:, :hf]) + nt(ag[b, 1, :, :hf], wg[:, hf:])
         grad = (grad + nt(ag[b, 1, :, hf:], wu[...])).astype(BF16)
         both = nn(put_x, out) + nn(put_y, grad)
         sbuf[pl.ds(b * ne, ne)] = both.reshape(ne, 8, wide).astype(BF16)
-        return carry
-
-    lax.fori_loop(0, nb, outputs, 0)
-    exchange(sbuf, bbuf, cb_send, cb_recv)
+
+        def send(i, carry):
+            o = lax.rem(i * 13, ne)
+            dc, r = lax.rem(o, nc), lax.div(o, nc)
+            dy, dz = lax.rem(r, ny), lax.div(r, ny)
+            pex = (lax.rem(zl + dz, nzl) * ny + lax.rem(yy + dy, ny)) * nc + lax.rem(core + dc, nc)
+            pltpu.make_async_remote_copy(
+                src_ref=sbuf.at[b * ne + pex], dst_ref=bbuf.at[me],
+                send_sem=cb_send, recv_sem=cb_recv.at[dp],
+                device_id=(b, pex), device_id_type=MESH,
+            ).start()
+            return carry
+
+        lax.fori_loop(first, ne, send, 0)
+
+    def outputs_beside(s):
+        def one(i, carry):
+            outputs(blk(lax.rem(x + 1 + 2 * i, nx), s), 0)
+            return carry
+
+        lax.fori_loop(0, 2, one, 0)
+
+    def ag_side(c, s):
+        for h in (0, 1):
+            wait_for(ag.at[blk(come[h], s), 1 - h], ag_recv.at[c, h, 1])
+
+    def ag_far(c, s):
+        for h in (0, 1):
+            wait_for(ag.at[blk(opposite, s), h], ag_recv.at[c, h, 2])
+
+    for h in (0, 1):
+        sends.append(remote(ag.at[dp, h], ag.at[dp, h], az_send.at[h], az_recv.at[h], zpeer))
+    ag_first(0, zh, 0)
+    ag_first(0, zh, 1)
+    outputs(dp, 1)
+    pltpu.make_async_copy(sbuf.at[me], bbuf.at[me], cb_recv.at[dp]).start()
+    ag_pass(0, zh)
+    ag_side(0, zh)
+    outputs_beside(zh)
+    wait_for(ag.at[zpeer, 0], az_recv.at[0])
+    ag_first(1, 1 - zh, 0)
+    ag_far(0, zh)
+    outputs(blk(opposite, zh), 0)
+    wait_for(ag.at[zpeer, 1], az_recv.at[1])
+    ag_first(1, 1 - zh, 1)
+    outputs(zpeer, 0)
+    ag_pass(1, 1 - zh)
+    ag_side(1, 1 - zh)
+    outputs_beside(1 - zh)
+    ag_far(1, 1 - zh)
+    outputs(blk(opposite, 1 - zh), 0)
 
     all_rows = nb * half
 
@@ -292,23 +324,28 @@
 
     lax.fori_loop(0, ff // 128, grads_down, 0)
 
-    arrived(bbuf, cb_recv)
-    tline = lax.broadcasted_iota(jnp.int32, (tdev, rows), 0)
-    to_out = tline == idx_row[...]
-    to_grad = (tline + tdev == idx_row[...]).astype(BF16)
-    weight = jnp.where(to_out, gate_row[...], 0.0)
+    here = lax.broadcasted_iota(jnp.int32, (tdev, half), 0) == pick_row[...]
+    to_grad = nn(here.astype(BF16), pick_y).astype(BF16)
+    weight = jnp.where(here, gate_row[...], 0.0)
     w_hi = weight.astype(BF16)
-    w_lo = (weight - w_hi.astype(F32)).astype(BF16)
-
-    def combine(k, prods):
+    w_lo = nn((weight - w_hi.astype(F32)).astype(BF16), pick_x).astype(BF16)
+    w_hi = nn(w_hi, pick_x).astype(BF16)
+
+    def combine(i, prods):
+        j = lax.rem(i, nx)
+        j = j + lax.div(j, 2) * (1 - 2 * lax.rem(j, 2))
+        s = lax.rem(zh + lax.div(i, nx), nzh)
+        k = blk(lax.rem(x + j, nx), s)
+        part = bbuf.at[pl.ds(k * ne, ne)]
+        pltpu.make_async_copy(part, part, cb_recv.at[k]).wait()
         at = pl.ds(pl.multiple_of(k * wide, 128), wide)
         z = bbuf[pl.ds(k * ne, ne)].reshape(rows, wide)
         mixed[:, at] = (nn(w_hi, z) + nn(w_lo, z)).astype(BF16)
         tgrad[:, at] = nn(to_grad, z).astype(BF16)
-        return prods + nt(z, cot[:, at])
-
-    prods = lax.fori_loop(0, nb, combine, jnp.zeros((rows, tdev), F32))
-    ggrad[...] = jnp.sum(jnp.where(lane == ids, prods, 0.0), axis=1, keepdims=True)
+        return prods + nt(cot[:, at], nn(pick_x, z).astype(BF16))
+
+    prods = lax.fori_loop(0, nb, combine, jnp.zeros((tdev, half), F32))
+    ggrad[...] = jnp.sum(jnp.where(here, prods, 0.0), axis=0, keepdims=True)
     for copy in sends:
         copy.wait_send()
     sent(sbuf, cb_send)
@@ -321,23 +358,19 @@
     n = nb * ne
     tdev, model = tokens.shape
     wide, ff = w_gate.shape[1], w_gate.shape[2]
-    rows, half, hw = ne * 8, ne * 4, 3 * ff // 2
-    chosen, scale = picks[0], gates[0]
-    idx = jnp.concatenate([chosen, chosen + tdev], axis=1)
-    weight = jnp.concatenate([jnp.ones_like(scale), scale], axis=1)
-    gate = jnp.concatenate([scale, scale], axis=1)
+    half, hw = ne * 4, 3 * ff // 2
     vm = pl.BlockSpec(memory_space=pltpu.VMEM)
     outs = pl.pallas_call(
         functools.partial(kernel, geo),
         out_shape=(
             jax.ShapeDtypeStruct((tdev, model), BF16),
             jax.ShapeDtypeStruct((tdev, model), BF16),
-            jax.ShapeDtypeStruct((rows, 1), F32),
+            jax.ShapeDtypeStruct((1, half), F32),
             jax.ShapeDtypeStruct((wide, ff), BF16),
             jax.ShapeDtypeStruct((wide, ff), BF16),
             jax.ShapeDtypeStruct((ff, wide), BF16),
         ),
-        in_specs=[vm] * 9,
+        in_specs=[vm] * 7,
         out_specs=(vm,) * 6,
         scratch_shapes=[
             pltpu.VMEM((n, 8, wide), BF16),
@@ -354,7 +387,7 @@
             pltpu.VMEM((nb, 2, half, hw), BF16),
             pltpu.VMEM((n, 8, wide), BF16),
             pltpu.SemaphoreType.DMA,
-            pltpu.SemaphoreType.DMA,
+            pltpu.SemaphoreType.DMA((nb,)),
             pltpu.SemaphoreType.DMA((2, 2, 3)),
             pltpu.SemaphoreType.DMA((2, 2, 3)),
             pltpu.SemaphoreType.DMA((2,)),
@@ -364,18 +397,18 @@
             pltpu.SemaphoreType.DMA((2,)),
             pltpu.SemaphoreType.DMA((2,)),
             pltpu.SemaphoreType.DMA,
-            pltpu.SemaphoreType.DMA,
+            pltpu.SemaphoreType.DMA((nb,)),
         ],
         compiler_params=pltpu.CompilerParams(
             collective_id=0, has_side_effects=True, vmem_limit_bytes=62 * 1024 * 1024
         ),
         name="moe",
     )(
-        tokens, cotangent, idx.reshape(rows, 1), weight.reshape(rows, 1),
-        idx.reshape(1, rows), gate.reshape(1, rows), w_gate[0], w_up[0], w_down[0],
+        tokens, cotangent, picks.reshape(1, half), gates.reshape(1, half),
+        w_gate[0], w_up[0], w_down[0],
     )
     mixed, tgrad, ggrad, gwg, gwu, gwd = outs
-    gate_grad = ggrad.reshape(ne, 8)[:, :slots].reshape(1, ne, slots)
+    gate_grad = ggrad.reshape(1, ne, slots)
     return (mixed, tgrad, gate_grad, gwg[None], gwu[None], gwd[None])
 
 

time: 283 us -> 228 us (0.81)
  Pallas kernels: 265 us -> 213 us
    pallas_call x1, Pallas kernels: 265 us -> 213 us  [body(): pl.pallas_call(functools.partial(kernel, geo), out_shape=(jax.ShapeDtypeS...]
    unnamed x14 -> x16, local copies, waits for them, and re-layouts: 9.05 us -> 10.5 us
where the time goes in v2:
time: 228 us; the launch traced here: 227 us
  Pallas kernels  213 us (93%)
  local copies, waits for them, and re-layouts  12.3 us (5%)
    pallas_call x1, Pallas kernels, body(): pl.pallas_call(functools.partial(kernel, geo), out_shape=(jax.ShapeDtypeS...  213 us
    unnamed x16, local copies, waits for them, and re-layouts  10.5 us

profile of v2, /device:TPU:1, one launch (start us, length us, event | category | flops | bytes accessed | tf_op | source)
XLA Modules:
  0.0 227.4 jit_solution(10775566206659127985)
XLA Ops:
  0.6 0.8 copy.16
  1.4 0.6 reshape.21.pick_row
  2.0 0.8 copy.17
  2.8 0.6 reshape.22.gate_row
  3.4 213.2 %moe.1 = (bf16[128,5120]{1,0:T(8,128)(2,1)}, bf16[128,5120]{1,0:T(8,128)(2,1)}, f32[1,128]{1,0:T(1,128)}, bf16[640,768]{1,0:T(8,128)(2,1)}, bf16[640,768]{1,0:T(8,128)(2,1)}, /*index=5*/bf16[768,640]{1,0:T(8,128)(2,1)}) custom-call(bf16[128,5120]{1,0:T(8,128)(2,1)} %tok.1, bf16[128,5120]{1,0:T(8,128)(2,1)} %cot.1, s32[1,128]{1,0:T(1,128)} %reshape.21.pick_row, ...), custom_call_target="tpu_custom_call" | custom-call | tf_op jit(solution)/shard_map/moe/pallas_call | solution.py:363
  216.6 0.5 broadcast.3
  217.1 1.3 reduce.3
  218.4 0.1 reshape.23
  218.5 0.7 copy.18
  219.1 0.0 copy-start
  219.1 2.6 %copy.24 = bf16[128,5120]{1,0:T(8,128)(2,1)} copy(bf16[128,5120]{1,0:T(8,128)(2,1)} %get-tuple-element.36) | data formatting | bytes 2621440
  221.7 0.0 copy-done
  221.7 0.0 copy-start.3
  221.7 1.1 copy.25
  222.8 0.6 copy-done.3
  223.4 0.0 copy-start.2
  223.4 0.9 copy.26
  224.3 0.6 copy-done.2
  224.9 0.0 copy-start.1
  224.9 0.9 copy.27
  225.9 0.6 copy-done.1
  226.5 0.9 copy.28
Async XLA Ops:
  219.1 2.6 %copy-start = (bf16[128,5120]{1,0:T(8,128)(2,1)S(1)}, bf16[128,5120]{1,0:T(8,128)(2,1)}, u32[]{:S(2)}) copy-start(bf16[128,5120]{1,0:T(8,128)(2,1)} %get-tuple-element.37) | copy-start | bytes 3932164
  221.7 1.7 copy-start.3
  223.4 1.6 copy-start.2
  224.9 1.6 copy-start.1

commit v3 on v2

--- a/solution.py
+++ b/solution.py
@@ -41,11 +41,12 @@
 
 def kernel(
     geo,
-    tok, cot, pick_row, gate_row, wg, wu, wd,
-    mixed, tgrad, ggrad, gwg, gwu, gwd,
-    sbuf, rbuf, xs, ys, terms, s1, t1, s2, s3, zb_out, fin, ag, bbuf,
-    a2a_send, a2a_recv, rs_send, rs_recv, z_send, z_recv, ag_send, ag_recv,
-    az_send, az_recv, cb_send, cb_recv,
+    tok_in, cot_in, pick_in, gate_in, wg_in, wu_in, wd_in,
+    mixed_out, tgrad_out, ggrad, gwg_out, gwu_out, gwd_out,
+    tok, cot, wg, wu, wd, mixed, tgrad, gwg, gwu, gwd,
+    sbuf, rbuf, xs, ys, terms, s1, t1, s2, s3, zb_out, ag, bbuf,
+    in_sem, out_sem, a2a_send, a2a_recv, rs_send, rs_recv, z_send, z_recv, ag_send, ag_recv,
+    cb_send, cb_recv,
 ):
     nx, nzh, nzl, ny, nc = geo
     ne = nzl * ny * nc
@@ -69,7 +70,15 @@
     zl = lax.div(ex, nc * ny)
     zz = zh * nzl + zl
 
+    loads = [
+        pltpu.make_async_copy(src, dst, in_sem.at[i])
+        for i, (src, dst) in enumerate(
+            ((tok_in, tok), (cot_in, cot), (wg_in, wg), (wu_in, wu), (wd_in, wd))
+        )
+    ]
     barrier = pltpu.get_barrier_semaphore()
+    for load in loads:
+        load.start()
 
     def greet(i, carry):
         other = lax.rem(me + i, n)
@@ -85,8 +94,29 @@
     eye = lax.broadcasted_iota(jnp.int32, (half, half), 0) == lax.broadcasted_iota(
         jnp.int32, (half, half), 1
     )
-    pick_col = jnp.sum(jnp.where(eye, pick_row[...], 0), axis=1, keepdims=True)
-    gate_col = jnp.sum(jnp.where(eye, gate_row[...], 0.0), axis=1, keepdims=True)
+    slot = lax.broadcasted_iota(jnp.int32, (4, half), 0) == lax.rem(
+        lax.broadcasted_iota(jnp.int32, (4, half), 1), 4
+    )
+    spread = (
+        lax.broadcasted_iota(jnp.int32, (ne, half), 0)
+        == lax.div(lax.broadcasted_iota(jnp.int32, (ne, half), 1), 4)
+    ).astype(BF16)
+
+    def pieces(v):
+        top = v.astype(BF16)
+        rest = v - top.astype(F32)
+        mid = rest.astype(BF16)
+        return top, mid, (rest - mid.astype(F32)).astype(BF16)
+
+    def in_row(v):
+        top, mid, low = pieces(v)
+        wide_v = nn(top, spread) + nn(mid, spread) + nn(low, spread)
+        return jnp.sum(jnp.where(slot, wide_v, 0.0), axis=0, keepdims=True)
+
+    pick_row = in_row(pick_in[...].astype(F32)).astype(jnp.int32)
+    gate_row = in_row(gate_in[...])
+    pick_col = jnp.sum(jnp.where(eye, pick_row, 0), axis=1, keepdims=True)
+    gate_col = jnp.sum(jnp.where(eye, gate_row, 0.0), axis=1, keepdims=True)
     hot = (lax.broadcasted_iota(jnp.int32, (half, tdev), 1) == pick_col).astype(BF16)
 
     def gather(k, carry):
@@ -97,6 +127,8 @@
         sbuf[pl.ds(k * ne, ne)] = both.reshape(ne, 8, wide).astype(BF16)
         return carry
 
+    loads[0].wait()
+    loads[1].wait()
     lax.fori_loop(0, nb, gather, 0)
     pl.semaphore_wait(barrier, n - 1)
 
@@ -146,7 +178,7 @@
     to = (lax.rem(x + 1, nx), lax.rem(x + nx - 1, nx))
     come = (to[1], to[0])
     opposite = lax.rem(x + 2, nx)
-    side = (1 - zh, zh)
+    side = (zh, 1 - zh)
 
     def blk(q, s):
         return q * nzh + s
@@ -193,6 +225,8 @@
         lax.fori_loop(0, count * nzh, one, 0)
 
     zpeer = blk(x, 1 - zh)
+    for load in loads[2:]:
+        load.wait()
     products_of(opposite, 0, 1)
     rs_first(0)
     rs_first(1)
@@ -200,36 +234,37 @@
     rs_pass(0)
     rs_pass(1)
     products_of(x, 0, 1)
-    for h in (0, 1):
-        zb_out[h] = rs_total(0, h).astype(BF16)
-        sends.append(remote(zb_out.at[h], s3.at[h], z_send.at[h], z_recv.at[h], zpeer))
-    for h in (0, 1):
-        fin[h] = rs_total(1, h)
+    for c in (0, 1):
+        for h in (0, 1):
+            zb_out[c, h] = rs_total(c, h).astype(BF16)
+            sends.append(remote(zb_out.at[c, h], s3.at[c, h], z_send.at[c, h], z_recv.at[c, h], zpeer))
     sent(sbuf, a2a_send)
-    for h in (0, 1):
-        wait_for(s3.at[h], z_recv.at[h])
 
     step = half // 4
 
-    def activate(i, carry):
-        at = pl.ds(pl.multiple_of(i * step, step), step)
-        lo = fin[0, at, :] + s3[0, at, :].astype(F32)
-        hi = fin[1, at, :] + s3[1, at, :].astype(F32)
-        gate = lo[:, :ff]
-        up = jnp.concatenate([lo[:, ff:], hi[:, :hf]], axis=1)
-        back = hi[:, hf:]
-        sig = 1.0 / (1.0 + jnp.exp(-gate))
-        silu = gate * sig
-        hidden = (silu * up).astype(BF16)
-        g_up = (back * silu).astype(BF16)
-        g_gate = (back * up * sig * (1.0 + gate * (1.0 - sig))).astype(BF16)
-        ag[dp, 0, at, :ff] = hidden
-        ag[dp, 0, at, ff:] = g_gate[:, :hf]
-        ag[dp, 1, at, :hf] = g_gate[:, hf:]
-        ag[dp, 1, at, hf:] = g_up
-        return carry
-
-    lax.fori_loop(0, 4, activate, 0)
+    def activate(b, c):
+        for h in (0, 1):
+            wait_for(s3.at[c, h], z_recv.at[c, h])
+
+        def part(i, carry):
+            at = pl.ds(pl.multiple_of(i * step, step), step)
+            lo = zb_out[1 - c, 0, at, :].astype(F32) + s3[c, 0, at, :].astype(F32)
+            hi = zb_out[1 - c, 1, at, :].astype(F32) + s3[c, 1, at, :].astype(F32)
+            gate = lo[:, :ff]
+            up = jnp.concatenate([lo[:, ff:], hi[:, :hf]], axis=1)
+            back = hi[:, hf:]
+            sig = 1.0 / (1.0 + jnp.exp(-gate))
+            silu = gate * sig
+            hidden = (silu * up).astype(BF16)
+            g_up = (back * silu).astype(BF16)
+            g_gate = (back * up * sig * (1.0 + gate * (1.0 - sig))).astype(BF16)
+            ag[b, 0, at, :ff] = hidden
+            ag[b, 0, at, ff:] = g_gate[:, :hf]
+            ag[b, 1, at, :hf] = g_gate[:, hf:]
+            ag[b, 1, at, hf:] = g_up
+            return carry
+
+        lax.fori_loop(0, 4, part, 0)
 
     def ag_first(c, s, g):
         mine = blk(x, s)
@@ -281,27 +316,25 @@
         for h in (0, 1):
             wait_for(ag.at[blk(opposite, s), h], ag_recv.at[c, h, 2])
 
-    for h in (0, 1):
-        sends.append(remote(ag.at[dp, h], ag.at[dp, h], az_send.at[h], az_recv.at[h], zpeer))
-    ag_first(0, zh, 0)
-    ag_first(0, zh, 1)
+    activate(zpeer, 0)
+    ag_first(0, 1 - zh, 0)
+    ag_first(0, 1 - zh, 1)
+    outputs(zpeer, 0)
+    ag_pass(0, 1 - zh)
+    ag_side(0, 1 - zh)
+    outputs_beside(1 - zh)
+    ag_far(0, 1 - zh)
+    outputs(blk(opposite, 1 - zh), 0)
+    activate(dp, 1)
+    ag_first(1, zh, 0)
+    ag_first(1, zh, 1)
     outputs(dp, 1)
     pltpu.make_async_copy(sbuf.at[me], bbuf.at[me], cb_recv.at[dp]).start()
-    ag_pass(0, zh)
-    ag_side(0, zh)
+    ag_pass(1, zh)
+    ag_side(1, zh)
     outputs_beside(zh)
-    wait_for(ag.at[zpeer, 0], az_recv.at[0])
-    ag_first(1, 1 - zh, 0)
-    ag_far(0, zh)
+    ag_far(1, zh)
     outputs(blk(opposite, zh), 0)
-    wait_for(ag.at[zpeer, 1], az_recv.at[1])
-    ag_first(1, 1 - zh, 1)
-    outputs(zpeer, 0)
-    ag_pass(1, 1 - zh)
-    ag_side(1, 1 - zh)
-    outputs_beside(1 - zh)
-    ag_far(1, 1 - zh)
-    outputs(blk(opposite, 1 - zh), 0)
 
     all_rows = nb * half
 
@@ -324,9 +357,16 @@
 
     lax.fori_loop(0, ff // 128, grads_down, 0)
 
-    here = lax.broadcasted_iota(jnp.int32, (tdev, half), 0) == pick_row[...]
+    stores = [
+        pltpu.make_async_copy(src, dst, out_sem.at[i])
+        for i, (src, dst) in enumerate(((gwg, gwg_out), (gwu, gwu_out), (gwd, gwd_out)))
+    ]
+    for store in stores:
+        store.start()
+
+    here = lax.broadcasted_iota(jnp.int32, (tdev, half), 0) == pick_row
     to_grad = nn(here.astype(BF16), pick_y).astype(BF16)
-    weight = jnp.where(here, gate_row[...], 0.0)
+    weight = jnp.where(here, gate_row, 0.0)
     w_hi = weight.astype(BF16)
     w_lo = nn((weight - w_hi.astype(F32)).astype(BF16), pick_x).astype(BF16)
     w_hi = nn(w_hi, pick_x).astype(BF16)
@@ -342,13 +382,36 @@
         z = bbuf[pl.ds(k * ne, ne)].reshape(rows, wide)
         mixed[:, at] = (nn(w_hi, z) + nn(w_lo, z)).astype(BF16)
         tgrad[:, at] = nn(to_grad, z).astype(BF16)
+        pltpu.make_async_copy(mixed.at[:, at], mixed_out.at[:, at], out_sem.at[3]).start()
+        pltpu.make_async_copy(tgrad.at[:, at], tgrad_out.at[:, at], out_sem.at[4]).start()
         return prods + nt(cot[:, at], nn(pick_x, z).astype(BF16))
 
     prods = lax.fori_loop(0, nb, combine, jnp.zeros((tdev, half), F32))
-    ggrad[...] = jnp.sum(jnp.where(here, prods, 0.0), axis=0, keepdims=True)
+    total = jnp.sum(jnp.where(here, prods, 0.0), axis=0, keepdims=True)
+    top, mid, low = pieces(jnp.where(slot, total, 0.0))
+    ggrad[...] = nt(top, spread) + nt(mid, spread) + nt(low, spread)
+    for store in stores:
+        store.wait()
+    pltpu.make_async_copy(mixed, mixed_out, out_sem.at[3]).wait()
+    pltpu.make_async_copy(tgrad, tgrad_out, out_sem.at[4]).wait()
     for copy in sends:
         copy.wait_send()
     sent(sbuf, cb_send)
+
+
+def hand_on(*refs):
+    count = (len(refs) - 2) // 3
+    ins, outs, bufs = refs[:count], refs[count : 2 * count], refs[2 * count : 3 * count]
+    in_sem, out_sem = refs[3 * count :]
+    loads = [pltpu.make_async_copy(ins[i], bufs[i], in_sem.at[i]) for i in range(count)]
+    stores = [pltpu.make_async_copy(bufs[i], outs[i], out_sem.at[i]) for i in range(count)]
+    for load in loads:
+        load.start()
+    for load, store in zip(loads, stores):
+        load.wait()
+        store.start()
+    for store in stores:
+        store.wait()
 
 
 def body(geo, tokens, cotangent, picks, gates, w_gate, w_up, w_down):
@@ -360,19 +423,31 @@
     wide, ff = w_gate.shape[1], w_gate.shape[2]
     half, hw = ne * 4, 3 * ff // 2
     vm = pl.BlockSpec(memory_space=pltpu.VMEM)
+    hbm = pl.BlockSpec(memory_space=pl.ANY)
+    results = (
+        jax.ShapeDtypeStruct((tdev, model), BF16),
+        jax.ShapeDtypeStruct((tdev, model), BF16),
+        jax.ShapeDtypeStruct((slots, ne), F32),
+        jax.ShapeDtypeStruct((wide, ff), BF16),
+        jax.ShapeDtypeStruct((wide, ff), BF16),
+        jax.ShapeDtypeStruct((ff, wide), BF16),
+    )
     outs = pl.pallas_call(
         functools.partial(kernel, geo),
-        out_shape=(
-            jax.ShapeDtypeStruct((tdev, model), BF16),
-            jax.ShapeDtypeStruct((tdev, model), BF16),
-            jax.ShapeDtypeStruct((1, half), F32),
-            jax.ShapeDtypeStruct((wide, ff), BF16),
-            jax.ShapeDtypeStruct((wide, ff), BF16),
-            jax.ShapeDtypeStruct((ff, wide), BF16),
-        ),
-        in_specs=[vm] * 7,
-        out_specs=(vm,) * 6,
+        out_shape=results,
+        in_specs=[hbm, hbm, vm, vm, hbm, hbm, hbm],
+        out_specs=(hbm, hbm, vm, hbm, hbm, hbm),
         scratch_shapes=[
+            pltpu.VMEM((tdev, model), BF16),
+            pltpu.VMEM((tdev, model), BF16),
+            pltpu.VMEM((wide, ff), BF16),
+            pltpu.VMEM((wide, ff), BF16),
+            pltpu.VMEM((ff, wide), BF16),
+            pltpu.VMEM((tdev, model), BF16),
+            pltpu.VMEM((tdev, model), BF16),
+            pltpu.VMEM((wide, ff), BF16),
+            pltpu.VMEM((wide, ff), BF16),
+            pltpu.VMEM((ff, wide), BF16),
             pltpu.VMEM((n, 8, wide), BF16),
             pltpu.VMEM((n, 8, wide), BF16),
             pltpu.VMEM((nb, half, wide), BF16),
@@ -381,21 +456,20 @@
             pltpu.VMEM((2, 2, 2, half, hw), BF16),
             pltpu.VMEM((2, 2, half, hw), BF16),
             pltpu.VMEM((2, 2, half, hw), BF16),
-            pltpu.VMEM((2, half, hw), BF16),
-            pltpu.VMEM((2, half, hw), BF16),
-            pltpu.VMEM((2, half, hw), F32),
+            pltpu.VMEM((2, 2, half, hw), BF16),
+            pltpu.VMEM((2, 2, half, hw), BF16),
             pltpu.VMEM((nb, 2, half, hw), BF16),
             pltpu.VMEM((n, 8, wide), BF16),
+            pltpu.SemaphoreType.DMA((5,)),
+            pltpu.SemaphoreType.DMA((5,)),
             pltpu.SemaphoreType.DMA,
             pltpu.SemaphoreType.DMA((nb,)),
             pltpu.SemaphoreType.DMA((2, 2, 3)),
             pltpu.SemaphoreType.DMA((2, 2, 3)),
-            pltpu.SemaphoreType.DMA((2,)),
-            pltpu.SemaphoreType.DMA((2,)),
+            pltpu.SemaphoreType.DMA((2, 2)),
+            pltpu.SemaphoreType.DMA((2, 2)),
             pltpu.SemaphoreType.DMA((2, 2, 3)),
             pltpu.SemaphoreType.DMA((2, 2, 3)),
-            pltpu.SemaphoreType.DMA((2,)),
-            pltpu.SemaphoreType.DMA((2,)),
             pltpu.SemaphoreType.DMA,
             pltpu.SemaphoreType.DMA((nb,)),
         ],
@@ -404,12 +478,21 @@
         ),
         name="moe",
     )(
-        tokens, cotangent, picks.reshape(1, half), gates.reshape(1, half),
+        tokens, cotangent, picks[0].T, gates[0].T,
         w_gate[0], w_up[0], w_down[0],
     )
+    outs = pl.pallas_call(
+        hand_on,
+        out_shape=results,
+        in_specs=[hbm] * 6,
+        out_specs=(hbm,) * 6,
+        scratch_shapes=[pltpu.VMEM(r.shape, r.dtype) for r in results]
+        + [pltpu.SemaphoreType.DMA((6,)), pltpu.SemaphoreType.DMA((6,))],
+        compiler_params=pltpu.CompilerParams(vmem_limit_bytes=62 * 1024 * 1024),
+        name="hand_on",
+    )(*outs)
     mixed, tgrad, ggrad, gwg, gwu, gwd = outs
-    gate_grad = ggrad.reshape(1, ne, slots)
-    return (mixed, tgrad, gate_grad, gwg[None], gwu[None], gwd[None])
+    return (mixed, tgrad, ggrad.T[None], gwg[None], gwu[None], gwd[None])
 
 
 def solution(mesh):

time: 228 us -> 217 us (0.952)
  local copies, waits for them, and re-layouts: 12.3 us -> 0 us
  Pallas kernels: 213 us -> 216 us
    unnamed x16 -> x0, local copies, waits for them, and re-layouts: 10.5 us -> none
    pallas_call x1 -> x2, Pallas kernels: 213 us -> 216 us  [the longest x1 212 us: body(): pl.pallas_call(functools.partial(kernel, geo), out_shape=results, in_spec...]
where the time goes in v3:
time: 217 us
  Pallas kernels  216 us (100%)
    pallas_call x1, Pallas kernels, body(): pl.pallas_call(functools.partial(kernel, geo), out_shape=results, in_spec...  212 us
    pallas_call x1, Pallas kernels, body(): pl.pallas_call(hand_on, out_shape=results, in_specs=[hbm] * 6, out_specs=...  4.49 us

profile of v3, /device:TPU:1, one launch (start us, length us, event | category | flops | bytes accessed | tf_op | source)
XLA Modules:
  0.0 216.6 jit_solution(3528510003112859385)
XLA Ops:
  0.6 211.5 %moe.1 = (bf16[128,5120]{1,0:T(8,128)(2,1)}, bf16[128,5120]{1,0:T(8,128)(2,1)}, f32[4,32]{1,0:T(4,128)}, bf16[640,768]{1,0:T(8,128)(2,1)}, bf16[640,768]{1,0:T(8,128)(2,1)}, /*index=5*/bf16[768,640]{1,0:T(8,128)(2,1)}) custom-call(bf16[128,5120]{1,0:T(8,128)(2,1)} %tok_in.1, bf16[128,5120]{1,0:T(8,128)(2,1)} %cot_in.1, s32[4,32]{1,0:T(4,128)} %bitcast.18, ...), custom_call_target="tpu_custom_call" | custom-call | tf_op jit(solution)/shard_map/moe/pallas_call | solution.py:435
  212.2 4.5 %hand_on.1 = (bf16[128,5120]{1,0:T(8,128)(2,1)}, bf16[128,5120]{1,0:T(8,128)(2,1)}, f32[4,32]{1,0:T(4,128)}, bf16[640,768]{1,0:T(8,128)(2,1)}, bf16[640,768]{1,0:T(8,128)(2,1)}, /*index=5*/bf16[768,640]{1,0:T(8,128)(2,1)}) custom-call(bf16[128,5120]{1,0:T(8,128)(2,1)} %get-tuple-element.18.refs_0_, bf16[128,5120]{1,0:T(8,128)(2,1)} %get-tuple-element.19.refs_1_, ...), custom_call_target="tpu_custom_call" | custom-call | tf_op jit(solution)/shard_map/hand_on/pallas_call | solution.py:484

commit v4 on v3

--- a/solution.py
+++ b/solution.py
@@ -225,6 +225,10 @@
         lax.fori_loop(0, count * nzh, one, 0)
 
     zpeer = blk(x, 1 - zh)
+
+    def z_exchange(c, h):
+        sends.append(remote(zb_out.at[c, h], s3.at[c, h], z_send.at[c, h], z_recv.at[c, h], zpeer))
+
     for load in loads[2:]:
         load.wait()
     products_of(opposite, 0, 1)
@@ -237,15 +241,16 @@
     for c in (0, 1):
         for h in (0, 1):
             zb_out[c, h] = rs_total(c, h).astype(BF16)
-            sends.append(remote(zb_out.at[c, h], s3.at[c, h], z_send.at[c, h], z_recv.at[c, h], zpeer))
+            if c == 0:
+                z_exchange(c, h)
+    for h in (0, 1):
+        wait_for(s3.at[0, h], z_recv.at[0, h])
+        z_exchange(1, h)
     sent(sbuf, a2a_send)
 
     step = half // 4
 
     def activate(b, c):
-        for h in (0, 1):
-            wait_for(s3.at[c, h], z_recv.at[c, h])
-
         def part(i, carry):
             at = pl.ds(pl.multiple_of(i * step, step), step)
             lo = zb_out[1 - c, 0, at, :].astype(F32) + s3[c, 0, at, :].astype(F32)
@@ -280,13 +285,14 @@
             sends.append(remote(ag.at[got, h], ag.at[got, h], ag_send.at[c, h, 2],
                                 ag_recv.at[c, h, 2], blk(to[h], zh)))
 
-    def outputs(b, first):
+    def outputs(b):
         out = nn(ag[b, 0, :, :ff], wd[...]).astype(BF16)
         grad = nt(ag[b, 0, :, ff:], wg[:, :hf]) + nt(ag[b, 1, :, :hf], wg[:, hf:])
         grad = (grad + nt(ag[b, 1, :, hf:], wu[...])).astype(BF16)
         both = nn(put_x, out) + nn(put_y, grad)
         sbuf[pl.ds(b * ne, ne)] = both.reshape(ne, 8, wide).astype(BF16)
 
+    def ship(b, first):
         def send(i, carry):
             o = lax.rem(i * 13, ne)
             dc, r = lax.rem(o, nc), lax.div(o, nc)
@@ -301,12 +307,16 @@
 
         lax.fori_loop(first, ne, send, 0)
 
-    def outputs_beside(s):
+    def beside(s, *steps):
         def one(i, carry):
-            outputs(blk(lax.rem(x + 1 + 2 * i, nx), s), 0)
+            for step in steps:
+                step(blk(lax.rem(x + 1 + 2 * i, nx), s))
             return carry
 
         lax.fori_loop(0, 2, one, 0)
+
+    def ship_all(b):
+        ship(b, 0)
 
     def ag_side(c, s):
         for h in (0, 1):
@@ -319,22 +329,29 @@
     activate(zpeer, 0)
     ag_first(0, 1 - zh, 0)
     ag_first(0, 1 - zh, 1)
-    outputs(zpeer, 0)
+    outputs(zpeer)
     ag_pass(0, 1 - zh)
     ag_side(0, 1 - zh)
-    outputs_beside(1 - zh)
+    beside(1 - zh, outputs)
     ag_far(0, 1 - zh)
-    outputs(blk(opposite, 1 - zh), 0)
+    outputs(blk(opposite, 1 - zh))
+    for h in (0, 1):
+        wait_for(s3.at[1, h], z_recv.at[1, h])
+    ship_all(zpeer)
     activate(dp, 1)
     ag_first(1, zh, 0)
     ag_first(1, zh, 1)
-    outputs(dp, 1)
+    beside(1 - zh, ship_all)
+    ship_all(blk(opposite, 1 - zh))
+    outputs(dp)
+    ship(dp, 1)
     pltpu.make_async_copy(sbuf.at[me], bbuf.at[me], cb_recv.at[dp]).start()
     ag_pass(1, zh)
     ag_side(1, zh)
-    outputs_beside(zh)
+    beside(zh, outputs, ship_all)
     ag_far(1, zh)
-    outputs(blk(opposite, zh), 0)
+    outputs(blk(opposite, zh))
+    ship_all(blk(opposite, zh))
 
     all_rows = nb * half
 

time: 217 us -> 213 us (0.982)
  Pallas kernels: 216 us -> 213 us
    pallas_call x1, Pallas kernels: 212 us -> 208 us  [body(): pl.pallas_call(functools.partial(kernel, geo), out_shape=results, in_spec...]
where the time goes in v4:
time: 213 us
  Pallas kernels  213 us (100%)
    pallas_call x1, Pallas kernels, body(): pl.pallas_call(functools.partial(kernel, geo), out_shape=results, in_spec...  208 us
    pallas_call x1, Pallas kernels, body(): pl.pallas_call(hand_on, out_shape=results, in_specs=[hbm] * 6, out_specs=...  4.49 us

profile of v4, /device:TPU:1, one launch (start us, length us, event | category | flops | bytes accessed | tf_op | source)
XLA Modules:
  0.0 213.2 jit_solution(15340305448242045058)
XLA Ops:
  0.6 208.0 %moe.1 = (bf16[128,5120]{1,0:T(8,128)(2,1)}, bf16[128,5120]{1,0:T(8,128)(2,1)}, f32[4,32]{1,0:T(4,128)}, bf16[640,768]{1,0:T(8,128)(2,1)}, bf16[640,768]{1,0:T(8,128)(2,1)}, /*index=5*/bf16[768,640]{1,0:T(8,128)(2,1)}) custom-call(bf16[128,5120]{1,0:T(8,128)(2,1)} %tok_in.1, bf16[128,5120]{1,0:T(8,128)(2,1)} %cot_in.1, s32[4,32]{1,0:T(4,128)} %bitcast.18, ...), custom_call_target="tpu_custom_call" | custom-call | tf_op jit(solution)/shard_map/moe/pallas_call | solution.py:452
  208.7 4.5 %hand_on.1 = (bf16[128,5120]{1,0:T(8,128)(2,1)}, bf16[128,5120]{1,0:T(8,128)(2,1)}, f32[4,32]{1,0:T(4,128)}, bf16[640,768]{1,0:T(8,128)(2,1)}, bf16[640,768]{1,0:T(8,128)(2,1)}, /*index=5*/bf16[768,640]{1,0:T(8,128)(2,1)}) custom-call(bf16[128,5120]{1,0:T(8,128)(2,1)} %get-tuple-element.18.refs_0_, bf16[128,5120]{1,0:T(8,128)(2,1)} %get-tuple-element.19.refs_1_, ...), custom_call_target="tpu_custom_call" | custom-call | tf_op jit(solution)/shard_map/hand_on/pallas_call | solution.py:501

commit v5 on v4

--- a/solution.py
+++ b/solution.py
@@ -154,7 +154,6 @@
 
     dispatch((2,), 0)
     dispatch((1, 3), 0)
-    dispatch((0,), 1)
     pltpu.make_async_copy(sbuf.at[me], rbuf.at[me], a2a_recv.at[dp]).start()
 
     def sent(src, send_sem):
@@ -234,6 +233,7 @@
     products_of(opposite, 0, 1)
     rs_first(0)
     rs_first(1)
+    dispatch((0,), 1)
     products_of(x + 1, 2, 2)
     rs_pass(0)
     rs_pass(1)
@@ -341,12 +341,12 @@
     activate(dp, 1)
     ag_first(1, zh, 0)
     ag_first(1, zh, 1)
+    outputs(dp)
+    ag_pass(1, zh)
     beside(1 - zh, ship_all)
     ship_all(blk(opposite, 1 - zh))
-    outputs(dp)
     ship(dp, 1)
     pltpu.make_async_copy(sbuf.at[me], bbuf.at[me], cb_recv.at[dp]).start()
-    ag_pass(1, zh)
     ag_side(1, zh)
     beside(zh, outputs, ship_all)
     ag_far(1, zh)

time: 213 us -> 218 us (1.023)
  Pallas kernels: 213 us -> 217 us
    pallas_call x1, Pallas kernels: 208 us -> 212 us  [body(): pl.pallas_call(functools.partial(kernel, geo), out_shape=results, in_spec...]
where the time goes in v5:
time: 218 us
  Pallas kernels  217 us (100%)
    pallas_call x1, Pallas kernels, body(): pl.pallas_call(functools.partial(kernel, geo), out_shape=results, in_spec...  212 us
    pallas_call x1, Pallas kernels, body(): pl.pallas_call(hand_on, out_shape=results, in_specs=[hbm] * 6, out_specs=...  4.49 us

profile of v5, /device:TPU:1, one launch (start us, length us, event | category | flops | bytes accessed | tf_op | source)
XLA Modules:
  0.0 217.5 jit_solution(13921860199605341302)
XLA Ops:
  0.6 212.4 %moe.1 = (bf16[128,5120]{1,0:T(8,128)(2,1)}, bf16[128,5120]{1,0:T(8,128)(2,1)}, f32[4,32]{1,0:T(4,128)}, bf16[640,768]{1,0:T(8,128)(2,1)}, bf16[640,768]{1,0:T(8,128)(2,1)}, /*index=5*/bf16[768,640]{1,0:T(8,128)(2,1)}) custom-call(bf16[128,5120]{1,0:T(8,128)(2,1)} %tok_in.1, bf16[128,5120]{1,0:T(8,128)(2,1)} %cot_in.1, s32[4,32]{1,0:T(4,128)} %bitcast.18, ...), custom_call_target="tpu_custom_call" | custom-call | tf_op jit(solution)/shard_map/moe/pallas_call | solution.py:452
  213.1 4.5 %hand_on.1 = (bf16[128,5120]{1,0:T(8,128)(2,1)}, bf16[128,5120]{1,0:T(8,128)(2,1)}, f32[4,32]{1,0:T(4,128)}, bf16[640,768]{1,0:T(8,128)(2,1)}, bf16[640,768]{1,0:T(8,128)(2,1)}, /*index=5*/bf16[768,640]{1,0:T(8,128)(2,1)}) custom-call(bf16[128,5120]{1,0:T(8,128)(2,1)} %get-tuple-element.18.refs_0_, bf16[128,5120]{1,0:T(8,128)(2,1)} %get-tuple-element.19.refs_1_, ...), custom_call_target="tpu_custom_call" | custom-call | tf_op jit(solution)/shard_map/hand_on/pallas_call | solution.py:501

commit v6 on v4

--- a/solution.py
+++ b/solution.py
@@ -217,12 +217,12 @@
         return (terms[blk(x, side[c]), h].astype(F32) + s1[c, h, 0].astype(F32)
                 + s2[c, h].astype(F32))
 
-    def products_of(first, gap, count):
+    def products_of(first, gap, count, s):
         def one(i, carry):
-            products(blk(lax.rem(first + gap * lax.div(i, nzh), nx), lax.rem(i, nzh)))
+            products(blk(lax.rem(first + gap * i, nx), s))
             return carry
 
-        lax.fori_loop(0, count * nzh, one, 0)
+        lax.fori_loop(0, count, one, 0)
 
     zpeer = blk(x, 1 - zh)
 
@@ -231,14 +231,14 @@
 
     for load in loads[2:]:
         load.wait()
-    products_of(opposite, 0, 1)
-    rs_first(0)
-    rs_first(1)
-    products_of(x + 1, 2, 2)
-    rs_pass(0)
-    rs_pass(1)
-    products_of(x, 0, 1)
     for c in (0, 1):
+        products_of(opposite, 0, 1, side[c])
+        rs_first(c)
+    for c in (0, 1):
+        products_of(x + 1, 2, 2, side[c])
+        rs_pass(c)
+    for c in (0, 1):
+        products_of(x, 0, 1, side[c])
         for h in (0, 1):
             zb_out[c, h] = rs_total(c, h).astype(BF16)
             if c == 0:
@@ -335,9 +335,9 @@
     beside(1 - zh, outputs)
     ag_far(0, 1 - zh)
     outputs(blk(opposite, 1 - zh))
-    for h in (0, 1):
-        wait_for(s3.at[1, h], z_recv.at[1, h])
+    wait_for(s3.at[1, 0], z_recv.at[1, 0])
     ship_all(zpeer)
+    wait_for(s3.at[1, 1], z_recv.at[1, 1])
     activate(dp, 1)
     ag_first(1, zh, 0)
     ag_first(1, zh, 1)
@@ -417,18 +417,14 @@
 
 
 def hand_on(*refs):
-    count = (len(refs) - 2) // 3
-    ins, outs, bufs = refs[:count], refs[count : 2 * count], refs[2 * count : 3 * count]
-    in_sem, out_sem = refs[3 * count :]
-    loads = [pltpu.make_async_copy(ins[i], bufs[i], in_sem.at[i]) for i in range(count)]
-    stores = [pltpu.make_async_copy(bufs[i], outs[i], out_sem.at[i]) for i in range(count)]
-    for load in loads:
-        load.start()
-    for load, store in zip(loads, stores):
-        load.wait()
-        store.start()
-    for store in stores:
-        store.wait()
+    count = (len(refs) - 1) // 2
+    copies = [
+        pltpu.make_async_copy(refs[i], refs[count + i], refs[-1].at[i]) for i in range(count)
+    ]
+    for copy in copies:
+        copy.start()
+    for copy in copies:
+        copy.wait()
 
 
 def body(geo, tokens, cotangent, picks, gates, w_gate, w_up, w_down):
@@ -441,6 +437,7 @@
     half, hw = ne * 4, 3 * ff // 2
     vm = pl.BlockSpec(memory_space=pltpu.VMEM)
     hbm = pl.BlockSpec(memory_space=pl.ANY)
+    far = pl.BlockSpec(memory_space=pltpu.HBM)
     results = (
         jax.ShapeDtypeStruct((tdev, model), BF16),
         jax.ShapeDtypeStruct((tdev, model), BF16),
@@ -452,7 +449,7 @@
     outs = pl.pallas_call(
         functools.partial(kernel, geo),
         out_shape=results,
-        in_specs=[hbm, hbm, vm, vm, hbm, hbm, hbm],
+        in_specs=[far, far, vm, vm, far, far, far],
         out_specs=(hbm, hbm, vm, hbm, hbm, hbm),
         scratch_shapes=[
             pltpu.VMEM((tdev, model), BF16),
@@ -491,21 +488,22 @@
             pltpu.SemaphoreType.DMA((nb,)),
         ],
         compiler_params=pltpu.CompilerParams(
-            collective_id=0, has_side_effects=True, vmem_limit_bytes=62 * 1024 * 1024
+            collective_id=0, has_side_effects=True, vmem_limit_bytes=46 * 1024 * 1024
         ),
         name="moe",
     )(
-        tokens, cotangent, picks[0].T, gates[0].T,
-        w_gate[0], w_up[0], w_down[0],
+        *(
+            pltpu.with_memory_space_constraint(v, pltpu.HBM)
+            for v in (tokens, cotangent, picks[0].T, gates[0].T, w_gate[0], w_up[0], w_down[0])
+        ),
     )
     outs = pl.pallas_call(
         hand_on,
         out_shape=results,
         in_specs=[hbm] * 6,
         out_specs=(hbm,) * 6,
-        scratch_shapes=[pltpu.VMEM(r.shape, r.dtype) for r in results]
-        + [pltpu.SemaphoreType.DMA((6,)), pltpu.SemaphoreType.DMA((6,))],
-        compiler_params=pltpu.CompilerParams(vmem_limit_bytes=62 * 1024 * 1024),
+        scratch_shapes=[pltpu.SemaphoreType.DMA((6,))],
+        compiler_params=pltpu.CompilerParams(vmem_limit_bytes=12 * 1024 * 1024),
         name="hand_on",
     )(*outs)
     mixed, tgrad, ggrad, gwg, gwu, gwd = outs

time: 213 us -> 212 us (level)
  no operation moved by 1% of the time
where the time goes in v6:
time: 212 us
  Pallas kernels  211 us (100%)
    pallas_call x1, Pallas kernels, body(): pl.pallas_call(functools.partial(kernel, geo), out_shape=results, in_spec...  209 us

profile of v6, /device:TPU:1, one launch (start us, length us, event | category | flops | bytes accessed | tf_op | source)
XLA Modules:
  0.0 212.0 jit_solution(13588784882600485479)
XLA Ops:
  0.6 208.9 %moe.1 = (bf16[128,5120]{1,0:T(8,128)(2,1)S(1)}, bf16[128,5120]{1,0:T(8,128)(2,1)S(1)}, f32[4,32]{1,0:T(4,128)S(1)}, bf16[640,768]{1,0:T(8,128)(2,1)S(1)}, bf16[...) custom-call(bf16[128,5120]{1,0:T(8,128)(2,1)} %tok_in.1, bf16[128,5120]{1,0:T(8,128)(2,1)} %cot_in.1, ...), custom_call_target="tpu_custom_call" | custom-call | tf_op jit(solution)/shard_map/moe/pallas_call | solution.py:449
  209.5 2.5 %hand_on.1 = (bf16[128,5120]{1,0:T(8,128)(2,1)}, bf16[128,5120]{1,0:T(8,128)(2,1)}, f32[4,32]{1,0:T(4,128)}, bf16[640,768]{1,0:T(8,128)(2,1)}, bf16[640,768]{1,0:T(8,128)(2,1)}, /*index=5*/bf16[768,640]{1,0:T(8,128)(2,1)}) custom-call(bf16[128,5120]{1,0:T(8,128)(2,1)S(1)} %get-tuple-element.18.refs_0_, bf16[128,5120]{1,0:T(8,128)(2,1)S(1)} %get-tuple-element.19.refs_1_, ...), custom_call_target="tpu_custom_call" | custom-call | tf_op jit(solution)/shard_map/hand_on/pallas_call | solution.py:500

commit v7 on v6

--- a/solution.py
+++ b/solution.py
@@ -241,11 +241,11 @@
         products_of(x, 0, 1, side[c])
         for h in (0, 1):
             zb_out[c, h] = rs_total(c, h).astype(BF16)
-            if c == 0:
+            if c == 0 or h == 0:
                 z_exchange(c, h)
-    for h in (0, 1):
-        wait_for(s3.at[0, h], z_recv.at[0, h])
-        z_exchange(1, h)
+    wait_for(s3.at[0, 0], z_recv.at[0, 0])
+    z_exchange(1, 1)
+    wait_for(s3.at[0, 1], z_recv.at[0, 1])
     sent(sbuf, a2a_send)
 
     step = half // 4

time: 212 us -> 212 us (level)
  no operation moved by 1% of the time
where the time goes in v7:
time: 212 us
  Pallas kernels  211 us (100%)
    pallas_call x1, Pallas kernels, body(): pl.pallas_call(functools.partial(kernel, geo), out_shape=results, in_spec...  209 us

profile of v7, /device:TPU:1, one launch (start us, length us, event | category | flops | bytes accessed | tf_op | source)
XLA Modules:
  0.0 211.9 jit_solution(5983349294263543438)
XLA Ops:
  0.6 208.7 %moe.1 = (bf16[128,5120]{1,0:T(8,128)(2,1)S(1)}, bf16[128,5120]{1,0:T(8,128)(2,1)S(1)}, f32[4,32]{1,0:T(4,128)S(1)}, bf16[640,768]{1,0:T(8,128)(2,1)S(1)}, bf16[...) custom-call(bf16[128,5120]{1,0:T(8,128)(2,1)} %tok_in.1, bf16[128,5120]{1,0:T(8,128)(2,1)} %cot_in.1, ...), custom_call_target="tpu_custom_call" | custom-call | tf_op jit(solution)/shard_map/moe/pallas_call | solution.py:449
  209.4 2.5 %hand_on.1 = (bf16[128,5120]{1,0:T(8,128)(2,1)}, bf16[128,5120]{1,0:T(8,128)(2,1)}, f32[4,32]{1,0:T(4,128)}, bf16[640,768]{1,0:T(8,128)(2,1)}, bf16[640,768]{1,0:T(8,128)(2,1)}, /*index=5*/bf16[768,640]{1,0:T(8,128)(2,1)}) custom-call(bf16[128,5120]{1,0:T(8,128)(2,1)S(1)} %get-tuple-element.18.refs_0_, bf16[128,5120]{1,0:T(8,128)(2,1)S(1)} %get-tuple-element.19.refs_1_, ...), custom_call_target="tpu_custom_call" | custom-call | tf_op jit(solution)/shard_map/hand_on/pallas_call | solution.py:500
